TPU v7x, 32 devices: a whole 2x2x4 slice. The times are simulated.
32 devices in a mesh: site: 8 (over z, x), task: 4 (over y, core).
Axes of the slice: x: 2, y: 2, z: 4, core: 2. Of those that a mesh axis runs over, the one named last changes fastest.
Arguments:
- values: bfloat16 [1024, 65536], P('task', 'site'), may hold values from -6 to 6
- factors: bfloat16 [1024, 128], P('task'), may hold values from -0.1875 to 0.1875
- jitter: bfloat16 [2, 65536], P(None, 'site'), may hold values from 0 to 1
- length_scales: float32 [4], replicated, may hold values from 1.1 to 2.5
- nugget: float32 [1024], P('task'), may hold values from 0.1 to 1
- neighbours: int32 [256, 3], P('site'), may hold values from -1 to 255, as said below
Outputs:
- product: float32 [1024, 65536], P('task', 'site')
Inputs may be any that keep to these rules, and one draw needn't show every extreme that they name: `neighbours`: row a is (a, (a - 1) mod 256, (a + 1) mod 256), where an entry is -1 if a barrier separates the two tiles; a barrier between tiles a and (a + 1) mod 256 removes each from the other's row.
All inputs are finite; a program needn't handle non-finite values.
Results may differ from a plain program's by a relative error of at most 0.0034.
Values may be sent and summed in bfloat16 or wider, within the bound.
No kernel may reach another device: no remote copies, remote signals or barrier semaphores. Data moves between devices by JAX's collectives and lax.ppermute only.
A program may use at most 64 MiB of HBM per device.

v0:
```python
import jax
import jax.numpy as jnp
from jax import lax
from jax.experimental import pallas as pl
from jax.experimental.pallas import tpu as pltpu
from jax.sharding import PartitionSpec as P


SIDE = 16
GROUP = 128
HALF = GROUP // 2
REACH = 3 * SIDE
KAPPA = 3.0**-0.25
FAR_AWAY = 1024.0
STEP = 512
EDGE_ROWS = 16
MIB = 1 << 20
CUTS = (8, 16, 23, 28)

VM = pl.BlockSpec(memory_space=pltpu.VMEM)
HBM = pl.BlockSpec(memory_space=pltpu.HBM)


def shape(dims, kind):
    return jax.ShapeDtypeStruct(dims, kind)


def in_hbm(x):
    return pltpu.with_memory_space_constraint(x, pltpu.HBM)


def grant(mib):
    return pltpu.CompilerParams(vmem_limit_bytes=mib * MIB)


def cost(flops, size):
    return pl.CostEstimate(flops=flops, bytes_accessed=size, transcendentals=0)


def tiles(groups, step=STEP):
    found, place = [], 0
    for begin, end in runs(groups):
        for at in range(begin * GROUP, end * GROUP, step):
            size = min(step, end * GROUP - at)
            found.append((at, place, size))
            place += size
    return found


def core_of():
    return lax.rem(lax.axis_index("task"), 2)


def columns(begin, size, side, span):
    return pl.ds(pl.multiple_of(side * span + begin, GROUP), size)


def project(values, factors, groups, resident):
    tasks, ranks = factors.shape
    span, width = values.shape[1] // 2, len(groups) * GROUP
    cuts = tiles(groups)

    def body(f_hbm, v_hbm, own_ref, send_ref, v_ref, f_ref, sems):
        core = core_of()
        first = pltpu.make_async_copy(f_hbm, f_ref, sems.at[2 * len(cuts)])
        first.start()
        work = [(send_ref, 1 - core, *cut) for cut in cuts] + [(own_ref, core, *cut) for cut in cuts]
        copies = [] if resident else [
            pltpu.make_async_copy(v_hbm.at[:, columns(at, size, side, span)], v_ref.at[i // len(cuts), :, pl.ds(place, size)], sems.at[i])
            for i, (_, side, at, place, size) in enumerate(work)
        ]
        for copy in copies:
            copy.start()
        first.wait()
        turned = f_ref[...].astype(jnp.float32).T.astype(jnp.bfloat16)
        for i, (out, side, at, place, size) in enumerate(work):
            s = slice(place, place + size)
            if resident:
                field = v_hbm[:, columns(at, size, side, span)]
            else:
                copies[i].wait()
                field = v_ref[i // len(cuts), :, s]
            out[:, s] = jnp.dot(turned, field, preferred_element_type=jnp.float32).astype(out.dtype)

    return pl.pallas_call(
        body,
        out_shape=(shape((ranks, width), jnp.float32), shape((ranks, width), jnp.bfloat16)),
        in_specs=[HBM, VM if resident else HBM],
        out_specs=(VM, VM),
        scratch_shapes=[
            pltpu.VMEM((1, 16, GROUP) if resident else (2, tasks, width), values.dtype),
            pltpu.VMEM(factors.shape, factors.dtype),
            pltpu.SemaphoreType.DMA((2 * len(cuts) + 1,)),
        ],
        compiler_params=grant(14),
        cost_estimate=cost(4 * tasks * ranks * width, tasks * width * 4),
        name="project",
    )(in_hbm(factors), values if resident else in_hbm(values))


def make_tables(jitter, neighbours, scales, nugget):
    span, owner, lat = jitter.shape[1] // 2, neighbours.shape[1], scales.shape[1]

    tasks = nugget.shape[1]

    def body(j_hbm, n_hbm, s_hbm, g_hbm, j_out, gap_out, beta_out, noise_out, n_ref, s_ref, g_ref, gap_ref, sems):
        core = core_of()
        copies = [
            pltpu.make_async_copy(j_hbm.at[:, columns(0, span, core, span)], j_out, sems.at[0]),
            pltpu.make_async_copy(n_hbm, n_ref, sems.at[1]),
            pltpu.make_async_copy(s_hbm, s_ref, sems.at[2]),
            pltpu.make_async_copy(g_hbm, g_ref, sems.at[3]),
        ]
        for copy in copies:
            copy.start()
        for copy in copies:
            copy.wait()
        noise_out[...] = jnp.broadcast_to(jnp.broadcast_to(g_ref[...], (8, tasks)).T[:, :1], (tasks, GROUP))
        lane = lax.broadcasted_iota(jnp.int32, (owner, GROUP), 1)
        for parity in range(2):
            cut = jnp.where(n_ref[parity + 1 : parity + 2, :] < 0, FAR_AWAY, 0.0)
            column = jnp.broadcast_to(cut, (8, owner)).T[:, :1]
            gap_ref[parity] = jnp.where((lane < HALF) == (parity == 0), jnp.broadcast_to(column, (owner, GROUP)), 0.0)
            mine = pl.multiple_of(core * (owner // 2), owner // 2)
            gap_out[parity] = gap_ref[parity, pl.ds(mine, owner // 2), :]
        scale = s_ref[...]
        which = lax.broadcasted_iota(jnp.int32, scale.shape, 1)
        beta = 1.0 / (KAPPA * scale * scale)
        for q in range(lat):
            value = jnp.sum(jnp.where(which == q, beta, 0.0), axis=1, keepdims=True)
            beta_out[8 * q : 8 * q + 8, :] = jnp.broadcast_to(value, (8, GROUP))

    return pl.pallas_call(
        body,
        out_shape=(
            shape((2, span), jitter.dtype),
            shape((2, owner // 2, GROUP), jnp.float32),
            shape((8 * lat, GROUP), jnp.float32),
            shape((tasks, GROUP), jnp.float32),
        ),
        in_specs=[HBM] * 4,
        out_specs=(VM, VM, VM, VM),
        scratch_shapes=[
            pltpu.VMEM(neighbours.shape, neighbours.dtype),
            pltpu.VMEM(scales.shape, scales.dtype),
            pltpu.VMEM(nugget.shape, nugget.dtype),
            pltpu.VMEM((2, owner, GROUP), jnp.float32),
            pltpu.SemaphoreType.DMA((4,)),
        ],
        compiler_params=grant(2),
        cost_estimate=cost(jitter.size, 4 * jitter.size),
        name="make_tables",
    )(in_hbm(jitter), in_hbm(neighbours), in_hbm(scales), in_hbm(nugget))


def add_cores(own, received, held, chunks):
    ranks = own.shape[0]

    def body(own_ref, got_ref, *outs):
        for groups, out in zip(chunks, outs):
            for begin, end in runs(groups):
                place = groups.index(begin) * GROUP
                s = slice(held.index(begin) * GROUP, held.index(end - 1) * GROUP + GROUP)
                total = own_ref[:, s] + got_ref[:, s].astype(jnp.float32)
                out[:, place : place + (end - begin) * GROUP] = total.astype(jnp.bfloat16)

    return pl.pallas_call(
        body,
        out_shape=[shape((ranks, len(groups) * GROUP), jnp.bfloat16) for groups in chunks],
        in_specs=[VM, VM],
        out_specs=[VM] * len(chunks),
        compiler_params=grant(8),
        cost_estimate=cost(own.size, own.size * 6),
        name="add_cores",
    )(own, received)


def take_edges(first, last, offsets):
    ranks = first.shape[0]

    def body(first_ref, last_ref, j_ref, *outs):
        for out, source, s in ((outs[0], first_ref, slice(0, GROUP)), (outs[1], last_ref, slice(-GROUP, None))):
            out[:ranks, :] = source[:, s]
            out[ranks:, :] = jnp.zeros((EDGE_ROWS, GROUP), jnp.bfloat16)
            out[ranks : ranks + 2, :] = j_ref[:, s]

    return pl.pallas_call(
        body,
        out_shape=[shape((ranks + EDGE_ROWS, GROUP), jnp.bfloat16)] * 2,
        in_specs=[VM] * 3,
        out_specs=[VM] * 2,
        compiler_params=grant(3),
        cost_estimate=cost(first.size, first.size),
        name="take_edges",
    )(first, last, offsets)


def close_ring(from_left, from_right, share):
    half, width = share.shape

    def body(left_ref, right_ref, share_ref, out, offsets):
        first_half = lax.broadcasted_iota(jnp.int32, (1, GROUP), 1) < HALF
        out[:, :width] = share_ref[...]
        out[:, width:] = jnp.where(first_half, right_ref[:half, :], left_ref[:half, :])
        offsets[...] = jnp.where(first_half, right_ref[half:, :], left_ref[half:, :])

    return pl.pallas_call(
        body,
        out_shape=(shape((half, width + GROUP), share.dtype), shape((EDGE_ROWS, GROUP), share.dtype)),
        in_specs=[VM, VM, VM],
        out_specs=(VM, VM),
        compiler_params=grant(2),
        cost_estimate=cost(share.size, 4 * share.size),
        name="close_ring",
    )(from_left, from_right, share)


def fill_blocks(region, groups, j_ref, gap_ref, beta_ref, edge_ref, k_ref):
    lat = beta_ref.shape[0] // 8
    rows = GROUP + REACH
    wide = 2 * GROUP
    sub = lax.broadcasted_iota(jnp.int32, (8, wide), 0)
    lane = lax.broadcasted_iota(jnp.int32, (8, wide), 1)
    row, col = ((lane >> 4).astype(jnp.float32), (lane & (SIDE - 1)).astype(jnp.float32))
    corner = lane >= GROUP
    past_row = jnp.where(corner, row - 11.0, row)
    zero = jnp.zeros_like(row)
    far_base = (
        jnp.where(sub == 1, past_row, jnp.where(sub == 4, row, jnp.where(sub >= 6, 1.0, zero))),
        jnp.where((sub == 1) | (sub == 4), col, jnp.where(sub >= 6, 1.0, zero)),
    )
    sub_1, lane_1 = sub[:, :GROUP], lane[:, :GROUP]
    meets = jnp.where((sub_1 < 3) == (lane_1 < HALF), 1.0, 0.0)
    own_base = tuple(jnp.where(sub_1 < 6, meets, -base[:, :GROUP]) for base in (row, col))
    none = jnp.zeros((8, GROUP), jnp.float32)
    first_half = lax.broadcasted_iota(jnp.int32, (1, GROUP), 1) < HALF
    scale = [beta_ref[8 * q : 8 * q + 1, :] for q in range(lat)]

    def offsets_of(b):
        if isinstance(b, int):
            return j_ref[:, b * GROUP : (b + 1) * GROUP].astype(jnp.float32)
        return j_ref[:, pl.ds(pl.multiple_of(b * GROUP, GROUP), GROUP)].astype(jnp.float32)

    def eight(x):
        return jnp.broadcast_to(x, (8, GROUP))

    def block(b, parity, slot):
        here = offsets_of(b)
        before = edge_ref[:2, :].astype(jnp.float32) if isinstance(b, int) and b == 0 else offsets_of(b - 1)
        after = edge_ref[:2, :].astype(jnp.float32) if isinstance(b, int) and b == groups - 1 else offsets_of(b + 1)
        gap = eight(gap_ref[parity, pl.ds(b // 2, 1), :])
        far, own = [], []
        for axis in range(2):
            mine = eight(here[axis : axis + 1])
            past = pltpu.roll(eight(before[axis : axis + 1]), REACH, 1)
            coming = eight(after[axis : axis + 1])
            base = far_base[axis]
            left = jnp.where((sub_1 == 0) | (sub_1 == 3), mine, base[:, :GROUP])
            right = jnp.where(sub_1 == 0, past, jnp.where(sub_1 == 3, coming, base[:, GROUP:]))
            if axis == 0 and parity == 0:
                right = jnp.where(sub_1 == 2, gap, right)
            if axis == 0 and parity == 1:
                right = jnp.where(sub_1 == 5, pltpu.roll(gap, HALF, 1), right)
            far.append(jnp.concatenate([left, right], axis=1))
            own.append(jnp.where(sub_1 == 6, -mine, own_base[axis]))
        left = jnp.concatenate(far, axis=0).T[:rows].astype(jnp.bfloat16)
        right = jnp.concatenate(
            [jnp.concatenate([own[0], none], axis=1), jnp.concatenate([none, own[1]], axis=1)], axis=0
        ).astype(jnp.bfloat16)
        away = jnp.dot(left, right, preferred_element_type=jnp.float32)
        across, sideways = away[:, :GROUP], away[:, GROUP:]
        distance = across * across + sideways * sideways
        for q in range(lat):
            u = jnp.maximum(1.0 / KAPPA - scale[q] * distance, 0.0)
            weight = (u * u * u * (4.0 * KAPPA**3 - u)).astype(jnp.bfloat16)
            s = slice(q * GROUP, (q + 1) * GROUP)
            blank = jnp.zeros((REACH, GROUP), jnp.bfloat16)
            k_ref[slot, :GROUP, s] = weight[:GROUP]
            k_ref[slot, GROUP : GROUP + REACH, s] = jnp.where(first_half, blank, weight[GROUP:])
            k_ref[slot, wide - REACH :, s] = jnp.where(first_half, weight[GROUP:], blank)
        k_ref[slot, GROUP + REACH : wide - REACH, :] = jnp.zeros((GROUP - 2 * REACH, lat * GROUP), jnp.bfloat16)

    count = 4
    for begin, end in runs(region):
        slot = region.index(begin)
        low, high = begin + (begin == 0), end - (end == groups)
        low = min(low + low % 2, end)
        for b in range(begin, low):
            block(b, b % 2, slot + b - begin)
        whole = (high - low) // count

        def several(i, carry, low=low, shift=slot - begin):
            for m in range(count):
                b = low + i * count + m
                block(b, m % 2, b + shift)
            return carry

        if whole > 1:
            lax.fori_loop(0, whole, several, 0)
        else:
            whole = 0
        for b in range(low + whole * count, end):
            block(b, b % 2, slot + b - begin)


def kernel_blocks(tables, edges, region, groups):
    args = list(tables) + ([edges] if edges is not None else [])

    def body(*refs):
        fill_blocks(region, groups, *refs[:3], refs[3], refs[-1])

    return pl.pallas_call(
        body,
        out_shape=block_shape(tables, region),
        in_specs=[VM] * len(args),
        out_specs=VM,
        compiler_params=grant(6),
        cost_estimate=block_cost(tables, region),
        name="kernel_blocks",
    )(*args)


def block_shape(tables, region):
    return shape((len(region), 2 * GROUP, tables[2].shape[0] // 8 * GROUP), jnp.bfloat16)


def block_cost(tables, region):
    size = block_shape(tables, region).size
    return cost(30 * size, 2 * size)


def smooth(kernels, region, pieces, lat, rank, groups):
    half = lat * rank
    owners = [(k, m) for k, kernel in enumerate(kernels) for m in range(kernel.shape[0])]

    def body(*refs):
        k_refs, refs = refs[: len(kernels)], refs[len(kernels) :]
        out = refs[-1]
        first_half = lax.broadcasted_iota(jnp.int32, (1, GROUP), 1) < HALF

        def part(group, which, rows):
            group = groups if group < 0 else group
            for n, (held, _) in enumerate(pieces):
                if group in held:
                    at = held.index(group) * GROUP
                    return refs[2 * n + which][rows, at : at + GROUP]

        for n, b in enumerate(region):
            for q in range(lat):
                rows = slice(q * rank, (q + 1) * rank)
                sides = [
                    jnp.concatenate(
                        [part(b, w, rows), jnp.where(first_half, part(b + 1, w, rows), part(b - 1, w, rows))], axis=1
                    )
                    for w in range(2)
                ]
                total = jnp.dot(
                    jnp.concatenate(sides, axis=0),
                    k_refs[owners[n][0]][owners[n][1], :, q * GROUP : (q + 1) * GROUP],
                    preferred_element_type=jnp.float32,
                )
                out[rows, n * GROUP : (n + 1) * GROUP] = (total[:rank] + total[rank:]).astype(jnp.bfloat16)

    arrays = [a for _, pair in pieces for a in pair]
    count = len(region) * GROUP
    return pl.pallas_call(
        body,
        out_shape=shape((half, count), jnp.bfloat16),
        in_specs=[VM] * (len(kernels) + len(arrays)),
        out_specs=VM,
        compiler_params=grant(8),
        cost_estimate=cost(8 * half * GROUP * count, 4 * GROUP * lat * count),
        name="smooth",
    )(*kernels, *arrays)


def mix(smoothed, factors, noise, values, product, region, mine, more=None):
    tasks = factors.shape[0]
    span, width = values.shape[1] // 2, len(region) * GROUP
    cuts = tiles(region, GROUP)

    def body(s_ref, f_ref, g_ref, v_ref, *rest):
        o_buf, sems = rest[-2:]
        o_hbm = rest[-4] if more else rest[-3]
        side = core_of() if mine else 1 - core_of()
        copies = []
        for i, (at, place, size) in enumerate(cuts):
            s, p = slice(place, place + size), columns(at, size, side, span)
            mixed = jnp.dot(f_ref[...], s_ref[:, s], preferred_element_type=jnp.float32)
            o_buf[:, s] = mixed + g_ref[...] * v_ref[:, p].astype(jnp.float32)
            copies.append(pltpu.make_async_copy(o_buf.at[:, pl.ds(place, size)], o_hbm.at[:, p], sems.at[i]))
            copies[-1].start()
        if more:
            fill_blocks(more[2], more[3], *rest[:3], rest[3], rest[-3])
        for copy in copies:
            copy.wait()

    args = [smoothed, factors, noise, values]
    out, out_specs = [shape(values.shape, jnp.float32)], [HBM]
    price = cost(2 * tasks * factors.shape[1] * width, tasks * width * 4)
    if more:
        args += list(more[0]) + ([more[1]] if more[1] is not None else [])
        out.append(block_shape(more[0], more[2]))
        out_specs.append(VM)
        built = block_cost(more[0], more[2])
        price = cost(price.flops + built.flops, price.bytes_accessed + built.bytes_accessed)
    specs = [VM] * len(args)
    alias = {}
    if product is not None:
        alias = {len(args): 0}
        args.append(product)
        specs.append(HBM)
    return pl.pallas_call(
        body,
        out_shape=out,
        in_specs=specs,
        out_specs=out_specs,
        scratch_shapes=[pltpu.VMEM((tasks, width), jnp.float32), pltpu.SemaphoreType.DMA((len(cuts),))],
        input_output_aliases=alias,
        compiler_params=grant(12),
        cost_estimate=price,
        name="mix",
    )(*args)


def runs(groups):
    found = []
    for g in groups:
        if found and found[-1][1] == g:
            found[-1][1] = g + 1
        else:
            found.append([g, g + 1])
    return found


def partners(size, bit):
    return [(i, i ^ bit) for i in range(size)]


def sum_fields(share, size):
    bit, other = 2, None
    while bit < size:
        if other is not None:
            share = (share.astype(jnp.float32) + other.astype(jnp.float32)).astype(jnp.bfloat16)
        other = lax.ppermute(share, "task", partners(size, bit))
        bit *= 2
    return share, other


def plan(groups):
    cuts = [1] + [groups * n // 32 for n in CUTS]
    regions = [list(range(a, b)) for a, b in zip(cuts[:-1], cuts[1:])]
    regions.append(list(range(cuts[-1], groups)) + [0])
    starts = [0] + [c + 1 for c in cuts[1:]] + [groups]
    chunks = [list(range(a, b)) for a, b in zip(starts[:-1], starts[1:])]
    return regions, chunks


def steps_of(values, factors, jitter, length_scales, nugget, neighbours):
    peers, blocks = lax.axis_size("task"), lax.axis_size("site")
    lat = length_scales.shape[0]
    rank = factors.shape[1] // lat
    groups = values.shape[1] // (2 * GROUP)
    regions, chunks = plan(groups)
    rest = [g for chunk in chunks[1:] for g in chunk]
    own, send = project(values, factors, chunks[0], False)
    received = lax.ppermute(send, "task", partners(peers, 1))
    *tables, noise = make_tables(jitter, neighbours.T, length_scales.reshape(1, -1), nugget.reshape(1, -1))
    (share,) = add_cores(own, received, chunks[0], chunks[:1])
    sums = [sum_fields(share, peers)]
    own, send = project(values, factors, rest, True)
    received = lax.ppermute(send, "task", partners(peers, 1))
    shares = add_cores(own, received, rest, chunks[1:])
    for part in shares[:-1]:
        sums.append(sum_fields(part, peers))
    left_edge, right_edge = take_edges(share, shares[-1], tables[0])
    ring = [[s * peers + t + c for s in range(blocks) for c in range(2)] for t in range(0, peers, 2)]
    up = [(r[i], r[(i + 1) % len(r)]) for r in ring for i in range(len(r))]
    down = [(j, i) for i, j in up]
    from_left = lax.ppermute(right_edge, ("site", "task"), up)
    from_right = lax.ppermute(left_edge, ("site", "task"), down)
    last, outside = close_ring(from_left, from_right, shares[-1])
    sums.append(sum_fields(last, peers))
    held_groups = chunks[:-1] + [chunks[-1] + [groups]]

    final = len(regions) - 1
    parts = dict(zip(("mix0", "mix0b", "mix1", "mix1b"), regions[1:]))
    kernels = [[] for _ in regions]
    kernels[0].append(kernel_blocks(tables, None, regions[0], groups))

    product = None
    for n, region in enumerate(regions):
        pieces = [(held_groups[n], sums[n])]
        if n > 0:
            pieces.append((held_groups[n - 1], sums[n - 1]))
        if n == final:
            pieces.append((held_groups[0], sums[0]))
        smoothed = smooth(kernels[n], region, pieces, lat, rank, groups)
        other = lax.ppermute(smoothed, "task", partners(peers, 1))
        for name, rows, mine in ((f"mix{n}", smoothed, True), (f"mix{n}b", other, False)):
            part = parts.get(name)
            more = part and (tables, outside if part is regions[final] else None, part, groups)
            product, *built = mix(rows, factors, noise, values, product, region, mine, more)
            if built:
                kernels[regions.index(part)].append(built[0])
    return product


def solution(mesh):
    return jax.shard_map(
        steps_of,
        mesh=mesh,
        in_specs=(
            P("task", "site"),
            P("task", None),
            P(None, "site"),
            P(),
            P("task"),
            P("site", None),
        ),
        out_specs=P("task", "site"),
        check_vma=False,
    )
```

profile of v0, /device:TPU:0, one launch (start us, length us, event | category | flops | bytes accessed | tf_op | source)
XLA Modules:
  0.0 47.2 jit_solution(5840996055380276873)
XLA Ops:
  0.0 2.2 %copy-done = bf16[256,8192]{1,0:T(8,128)(2,1)S(1)} copy-done((bf16[256,8192]{1,0:T(8,128)(2,1)S(1)}, bf16[256,8192]{1,0:T(8,128)(2,1)}, u32[]{:S(2)}) %copy-start) | copy-done | bytes 4194328
  2.2 1.7 %project.3 = (f32[128,2944]{1,0:T(8,128)S(1)}, bf16[128,2944]{1,0:T(8,128)(2,1)S(1)}) custom-call(bf16[256,128]{1,0:T(8,128)(2,1)} %f_ref.19, bf16[256,8192]{1,0:T(8,128)(2,1)S(1)} %copy-done), custom_call_target="tpu_custom_call" | custom-call | flops 385875968 | bytes 3014656 | tf_op jit(solution)/shard_map/project/pallas_call | solution.py:85
  4.5 2.1 %project.2 = (f32[128,1152]{1,0:T(8,128)S(1)}, bf16[128,1152]{1,0:T(8,128)(2,1)S(1)}) custom-call(bf16[256,128]{1,0:T(8,128)(2,1)} %f_ref.19, bf16[256,8192]{1,0:T(8,128)(2,1)} %v_ref.19), custom_call_target="tpu_custom_call" | custom-call | flops 150994944 | bytes 1179648 | tf_op jit(solution)/shard_map/project/pallas_call | solution.py:85
  6.7 1.6 %collective-permute-done.got_ref = bf16[128,1152]{1,0:T(8,128)(2,1)S(1)} collective-permute-done((bf16[128,1152]{1,0:T(8,128)(2,1)S(1)}, bf16[128,1152]{1,0:T(8,128)(2,1)S(1)}, u32[]{:S(2)}, u32[]{:S(2)}) %collective-permute-start) | collective-permute-done | bytes 294944 | tf_op jit(solution)/shard_map/ppermute | solution.py:467
  8.4 2.7 %collective-permute-start.1 = (bf16[128,1152]{1,0:T(8,128)(2,1)S(1)}, bf16[128,1152]{1,0:T(8,128)(2,1)S(1)}, u32[]{:S(2)}, u32[]{:S(2)}) collective-permute-start(bf16[128,1152]{1,0:T(8,128)(2,1)S(1)} %add_cores.2.refs_1_.refs_3_.first_ref.refs_5_), channel_id=1, source_target_pairs={{0,2},{1,3},{2,0},{3,1},{4,6},{5,7},{6,4},{7,5},{8,10},{9,11},{10,... | collective-permute-start | bytes 884744 | tf_op jit(solution)/shard_map/ppermute | solution.py:445
  11.3 1.0 %make_tables.1 = (bf16[2,4096]{1,0:T(2,128)(2,1)S(1)}, f32[2,16,128]{2,1,0:T(8,128)S(1)}, f32[32,128]{1,0:T(8,128)S(1)}, f32[256,128]{1,0:T(8,128)S(1)}) custom-call(bf16[2,8192]{1,0:T(2,128)(2,1)} %j_hbm.1, s32[3,32]{1,0:T(4,128)} %bitcast.3, f32[1,4]{1,0:T(1,128)} %bitcast.5, f32[1,256]{1,0:T(1,128)} %bitcast.4), custom_call_target="tpu_custom_call" | custom-call | flops 16384 | bytes 65536 | tf_op jit(solution)/shard_map/make_tables/pallas_call | solution.py:133
  12.3 1.1 %kernel_blocks.1.refs_0_ = bf16[7,256,512]{2,1,0:T(8,128)(2,1)S(1)} custom-call(bf16[2,4096]{1,0:T(2,128)(2,1)S(1)} %get-tuple-element.29.refs_0_.rest_0_.j_ref, f32[2,16,128]{2,1,0:T(8,128)S(1)} %get-tuple-element.30.refs_1_.rest_1_, f32[32,128]{1,0:T(8,128)S(1)} %get-tuple-element.31.refs_2_.rest_2_), custom_call_target="tpu_custom_call" | custom-call | flops 27525120 | bytes 1835008 | tf_op jit(solution)/shard_map/kernel_blocks/pallas_call | solution.py:312
  13.4 5.5 %collective-permute-done.1.refs_2_.refs_4_.refs_6_ = bf16[128,1152]{1,0:T(8,128)(2,1)S(1)} collective-permute-done((bf16[128,1152]{1,0:T(8,128)(2,1)S(1)}, bf16[128,1152]{1,0:T(8,128)(2,1)S(1)}, u32[]{:S(2)}, u32[]{:S(2)}) %collective-permute-start.1) | collective-permute-done | bytes 294944 | tf_op jit(solution)/shard_map/ppermute | solution.py:445
  19.4 2.1 %collective-permute-start.11 = (bf16[128,896]{1,0:T(8,128)(2,1)S(1)}, bf16[128,896]{1,0:T(8,128)(2,1)S(1)}, u32[]{:S(2)}, u32[]{:S(2)}) collective-permute-start(bf16[128,896]{1,0:T(8,128)(2,1)S(1)} %get-tuple-element.50.refs_3_.refs_1_), channel_id=1, source_target_pairs={{0,2},{1,3},{2,0},{3,1},{4,6},{5,7},{6,4},{7,5},{8,10},{9,11},{10,... | collective-permute-start | bytes 688136 | tf_op jit(solution)/shard_map/ppermute | solution.py:445
  21.5 1.8 %mix.10 = (f32[256,8192]{1,0:T(8,128)}, bf16[8,256,512]{2,1,0:T(8,128)(2,1)S(1)}) custom-call(bf16[128,896]{1,0:T(8,128)(2,1)S(1)} %smooth.5.s_ref, bf16[256,128]{1,0:T(8,128)(2,1)S(1)} %copy-done.2, f32[256,128]{1,0:T(8,128)S(1)} %get-tuple-element.34.g_ref, bf16[256,8192]{1,0:T(8,128)(2,1)S(1)} %copy-done.1, ...), custom_call_target="tpu_custom_call" | custom-call | flops 90177536 | bytes 3014656 | tf_op jit(solution)/shard_map/mix/pallas_call | solution.py:413
  23.3 1.2 %collective-permute-done.3.refs_2_.refs_4_ = bf16[128,1024]{1,0:T(8,128)(2,1)S(1)} collective-permute-done((bf16[128,1024]{1,0:T(8,128)(2,1)S(1)}, bf16[128,1024]{1,0:T(8,128)(2,1)S(1)}, u32[]{:S(2)}, u32[]{:S(2)}) %collective-permute-start.3) | collective-permute-done | bytes 262176 | tf_op jit(solution)/shard_map/ppermute | solution.py:445
  25.6 2.0 %collective-permute-start.9 = (bf16[128,640]{1,0:T(8,128)(2,1)S(1)}, bf16[128,640]{1,0:T(8,128)(2,1)S(1)}, u32[]{:S(2)}, u32[]{:S(2)}) collective-permute-start(bf16[128,640]{1,0:T(8,128)(2,1)S(1)} %get-tuple-element.48.refs_3_.refs_1_), channel_id=1, source_target_pairs={{0,2},{1,3},{2,0},{3,1},{4,6},{5,7},{6,4},{7,5},{8,10},{9,11},{10,... | collective-permute-start | bytes 491528 | tf_op jit(solution)/shard_map/ppermute | solution.py:445
  27.6 4.3 %collective-permute-done.5.left_ref = bf16[144,128]{1,0:T(8,128)(2,1)S(1)} collective-permute-done((bf16[144,128]{1,0:T(8,128)(2,1)S(1)}, bf16[144,128]{1,0:T(8,128)(2,1)S(1)}, u32[]{:S(2)}, u32[]{:S(2)}) %collective-permute-start.5) | collective-permute-done | bytes 36896 | tf_op jit(solution)/shard_map/ppermute | solution.py:480
  31.9 1.6 %collective-permute-done.6.right_ref = bf16[144,128]{1,0:T(8,128)(2,1)S(1)} collective-permute-done((bf16[144,128]{1,0:T(8,128)(2,1)S(1)}, bf16[144,128]{1,0:T(8,128)(2,1)S(1)}, u32[]{:S(2)}, u32[]{:S(2)}) %collective-permute-start.6) | collective-permute-done | bytes 36896 | tf_op jit(solution)/shard_map/ppermute | solution.py:481
  33.6 1.6 %collective-permute-start.8 = (bf16[128,512]{1,0:T(8,128)(2,1)S(1)}, bf16[128,512]{1,0:T(8,128)(2,1)S(1)}, u32[]{:S(2)}, u32[]{:S(2)}) collective-permute-start(bf16[128,512]{1,0:T(8,128)(2,1)S(1)} %get-tuple-element.47.refs_1_), channel_id=1, source_target_pairs={{0,2},{1,3},{2,0},{3,1},{4,6},{5,7},{6,4},{7,5},{8,10},{9,11},{10,... | collective-permute-start | bytes 393224 | tf_op jit(solution)/shard_map/ppermute | solution.py:445
  35.1 1.3 %mix.11 = (f32[256,8192]{1,0:T(8,128)}, bf16[7,256,512]{2,1,0:T(8,128)(2,1)S(1)}) custom-call(bf16[128,896]{1,0:T(8,128)(2,1)S(1)} %collective-permute-done.7.s_ref, bf16[256,128]{1,0:T(8,128)(2,1)S(1)} %copy-done.2, f32[256,128]{1,0:T(8,128)S(1)} %get-tuple-element.34.g_ref, bf16[256,8192]{1,0:T(8,128)(2,1)S(1)} %copy-done.1, ...), custom_call_target="tpu_custom_call", output_to_operand_aliasing={{0}: (7, {})} | custom-call | flops 86245376 | bytes 2752512 | tf_op jit(solution)/shard_map/mix/pallas_call | solution.py:413
  36.9 1.2 %mix.12 = (f32[256,8192]{1,0:T(8,128)}, bf16[5,256,512]{2,1,0:T(8,128)(2,1)S(1)}) custom-call(bf16[128,1024]{1,0:T(8,128)(2,1)S(1)} %smooth.6.s_ref, bf16[256,128]{1,0:T(8,128)(2,1)S(1)} %copy-done.2, f32[256,128]{1,0:T(8,128)S(1)} %get-tuple-element.34.g_ref, bf16[256,8192]{1,0:T(8,128)(2,1)S(1)} %copy-done.1, ...), custom_call_target="tpu_custom_call", output_to_operand_aliasing={{0}: (7, {})} | custom-call | flops 86769664 | bytes 2359296 | tf_op jit(solution)/shard_map/mix/pallas_call | solution.py:413
  39.0 1.3 %mix.13 = (f32[256,8192]{1,0:T(8,128)}, bf16[5,256,512]{2,1,0:T(8,128)(2,1)S(1)}) custom-call(bf16[128,1024]{1,0:T(8,128)(2,1)S(1)} %collective-permute-done.4.s_ref, bf16[256,128]{1,0:T(8,128)(2,1)S(1)} %copy-done.2, f32[256,128]{1,0:T(8,128)S(1)} %get-tuple-element.34.g_ref, bf16[256,8192]{1,0:T(8,128)(2,1)S(1)} %copy-done.1, ...), custom_call_target="tpu_custom_call", output_to_operand_aliasing={{0}: (8, {})} | custom-call | flops 86769664 | bytes 2359296 | tf_op jit(solution)/shard_map/mix/pallas_call | solution.py:413
  40.7 1.1 %mix.14.rest_0_ = f32[256,8192]{1,0:T(8,128)} custom-call(bf16[128,896]{1,0:T(8,128)(2,1)S(1)} %smooth.9.s_ref, bf16[256,128]{1,0:T(8,128)(2,1)S(1)} %copy-done.2, f32[256,128]{1,0:T(8,128)S(1)} %get-tuple-element.34.g_ref, bf16[256,8192]{1,0:T(8,128)(2,1)S(1)} %copy-done.1, f32[256,8192]{1,0:T(8,128)} %get-tuple-element.52.rest_0_), custom_call_target="tpu_custom_call", output_to_operand_aliasing={{}: (4, {})} | custom-call | flops 58720256 | bytes 917504 | tf_op jit(solution)/shard_map/mix/pallas_call | solution.py:413
  41.9 1.2 %mix.15.rest_0_ = f32[256,8192]{1,0:T(8,128)} custom-call(bf16[128,896]{1,0:T(8,128)(2,1)S(1)} %collective-permute-done.13.s_ref, bf16[256,128]{1,0:T(8,128)(2,1)S(1)} %copy-done.2, f32[256,128]{1,0:T(8,128)S(1)} %get-tuple-element.34.g_ref, bf16[256,8192]{1,0:T(8,128)(2,1)S(1)} %copy-done.1, f32[256,8192]{1,0:T(8,128)} %mix.14.rest_0_), custom_call_target="tpu_custom_call", output_to_operand_aliasing={{}: (4, {})} | custom-call | flops 58720256 | bytes 917504 | tf_op jit(solution)/shard_map/mix/pallas_call | solution.py:413
  43.1 1.0 %mix.16.rest_0_ = f32[256,8192]{1,0:T(8,128)} custom-call(bf16[128,640]{1,0:T(8,128)(2,1)S(1)} %smooth.8.s_ref, bf16[256,128]{1,0:T(8,128)(2,1)S(1)} %copy-done.2, f32[256,128]{1,0:T(8,128)S(1)} %get-tuple-element.34.g_ref, bf16[256,8192]{1,0:T(8,128)(2,1)S(1)} %copy-done.1, f32[256,8192]{1,0:T(8,128)} %mix.15.rest_0_), custom_call_target="tpu_custom_call", output_to_operand_aliasing={{}: (4, {})} | custom-call | flops 41943040 | bytes 655360 | tf_op jit(solution)/shard_map/mix/pallas_call | solution.py:413
  44.1 1.0 %mix.17.rest_0_ = f32[256,8192]{1,0:T(8,128)} custom-call(bf16[128,640]{1,0:T(8,128)(2,1)S(1)} %collective-permute-done.12.s_ref, bf16[256,128]{1,0:T(8,128)(2,1)S(1)} %copy-done.2, f32[256,128]{1,0:T(8,128)S(1)} %get-tuple-element.34.g_ref, bf16[256,8192]{1,0:T(8,128)(2,1)S(1)} %copy-done.1, f32[256,8192]{1,0:T(8,128)} %mix.16.rest_0_), custom_call_target="tpu_custom_call", output_to_operand_aliasing={{}: (4, {})} | custom-call | flops 41943040 | bytes 655360 | tf_op jit(solution)/shard_map/mix/pallas_call | solution.py:413
  45.2 1.0 %mix.18.rest_0_ = f32[256,8192]{1,0:T(8,128)} custom-call(bf16[128,640]{1,0:T(8,128)(2,1)S(1)} %smooth.7.s_ref, bf16[256,128]{1,0:T(8,128)(2,1)S(1)} %copy-done.2, f32[256,128]{1,0:T(8,128)S(1)} %get-tuple-element.34.g_ref, bf16[256,8192]{1,0:T(8,128)(2,1)S(1)} %copy-done.1, f32[256,8192]{1,0:T(8,128)} %mix.17.rest_0_), custom_call_target="tpu_custom_call", output_to_operand_aliasing={{}: (4, {})} | custom-call | flops 41943040 | bytes 655360 | tf_op jit(solution)/shard_map/mix/pallas_call | solution.py:413
  46.2 1.0 %mix.19 = f32[256,8192]{1,0:T(8,128)} custom-call(bf16[128,640]{1,0:T(8,128)(2,1)S(1)} %collective-permute-done.10.s_ref, bf16[256,128]{1,0:T(8,128)(2,1)S(1)} %copy-done.2, f32[256,128]{1,0:T(8,128)S(1)} %get-tuple-element.34.g_ref, bf16[256,8192]{1,0:T(8,128)(2,1)S(1)} %copy-done.1, f32[256,8192]{1,0:T(8,128)} %mix.18.rest_0_), custom_call_target="tpu_custom_call", output_to_operand_aliasing={{}: (4, {})} | custom-call | flops 41943040 | bytes 655360 | tf_op jit(solution)/shard_map/mix/pallas_call | solution.py:413
  (33 shorter events, 4.3 us)
Async XLA Ops:
  0.0 2.2 %copy-start = (bf16[256,8192]{1,0:T(8,128)(2,1)S(1)}, bf16[256,8192]{1,0:T(8,128)(2,1)}, u32[]{:S(2)}) copy-start(bf16[256,8192]{1,0:T(8,128)(2,1)} %v_ref.19) | copy-start | bytes 12582916
  2.2 19.3 %copy-start.1 = (bf16[256,8192]{1,0:T(8,128)(2,1)S(1)}, bf16[256,8192]{1,0:T(8,128)(2,1)}, u32[]{:S(2)}) copy-start(bf16[256,8192]{1,0:T(8,128)(2,1)} %v_ref.19) | copy-start | bytes 12582916
  2.2 19.3 %copy-start.2 = (bf16[256,128]{1,0:T(8,128)(2,1)S(1)}, bf16[256,128]{1,0:T(8,128)(2,1)}, u32[]{:S(2)}) copy-start(bf16[256,128]{1,0:T(8,128)(2,1)} %f_ref.19) | copy-start | bytes 196612
  3.9 7.1 %collective-permute-start.2 = (bf16[128,2944]{1,0:T(8,128)(2,1)S(1)}, bf16[128,2944]{1,0:T(8,128)(2,1)S(1)}, u32[]{:S(2)}, u32[]{:S(2)}) collective-permute-start(bf16[128,2944]{1,0:T(8,128)(2,1)S(1)} %get-tuple-element.37), channel_id=1, source_target_pairs={{0,1},{1,0},{2,3},{3,2},{4,5},{5,4},{6,7},{7,6},{8,9},{9,8},{10,11... | collective-permute-start | bytes 2261000 | tf_op jit(solution)/shard_map/ppermute | solution.py:472
  6.7 1.6 %collective-permute-start = (bf16[128,1152]{1,0:T(8,128)(2,1)S(1)}, bf16[128,1152]{1,0:T(8,128)(2,1)S(1)}, u32[]{:S(2)}, u32[]{:S(2)}) collective-permute-start(bf16[128,1152]{1,0:T(8,128)(2,1)S(1)} %get-tuple-element.33), channel_id=1, source_target_pairs={{0,1},{1,0},{2,3},{3,2},{4,5},{5,4},{6,7},{7,6},{8,9},{9,8},{10,11... | collective-permute-start | bytes 884744 | tf_op jit(solution)/shard_map/ppermute | solution.py:467
  8.4 10.6 %collective-permute-start.1 = (bf16[128,1152]{1,0:T(8,128)(2,1)S(1)}, bf16[128,1152]{1,0:T(8,128)(2,1)S(1)}, u32[]{:S(2)}, u32[]{:S(2)}) collective-permute-start(bf16[128,1152]{1,0:T(8,128)(2,1)S(1)} %add_cores.2.refs_1_.refs_3_.first_ref.refs_5_), channel_id=1, source_target_pairs={{0,2},{1,3},{2,0},{3,1},{4,6},{5,7},{6,4},{7,5},{8,10},{9,11},{10,... | collective-permute-start | bytes 884744 | tf_op jit(solution)/shard_map/ppermute | solution.py:445
  11.2 13.3 %collective-permute-start.3 = (bf16[128,1024]{1,0:T(8,128)(2,1)S(1)}, bf16[128,1024]{1,0:T(8,128)(2,1)S(1)}, u32[]{:S(2)}, u32[]{:S(2)}) collective-permute-start(bf16[128,1024]{1,0:T(8,128)(2,1)S(1)} %get-tuple-element.38.refs_1_.refs_3_), channel_id=1, source_target_pairs={{0,2},{1,3},{2,0},{3,1},{4,6},{5,7},{6,4},{7,5},{8,10},{9,11},{10,... | collective-permute-start | bytes 786440 | tf_op jit(solution)/shard_map/ppermute | solution.py:445
  19.3 15.8 %collective-permute-start.7 = (bf16[128,896]{1,0:T(8,128)(2,1)S(1)}, bf16[128,896]{1,0:T(8,128)(2,1)S(1)}, u32[]{:S(2)}, u32[]{:S(2)}) collective-permute-start(bf16[128,896]{1,0:T(8,128)(2,1)S(1)} %smooth.5.s_ref), channel_id=1, source_target_pairs={{0,1},{1,0},{2,3},{3,2},{4,5},{5,4},{6,7},{7,6},{8,9},{9,8},{10,11... | collective-permute-start | bytes 688136 | tf_op jit(solution)/shard_map/ppermute | solution.py:499
  19.4 17.0 %collective-permute-start.11 = (bf16[128,896]{1,0:T(8,128)(2,1)S(1)}, bf16[128,896]{1,0:T(8,128)(2,1)S(1)}, u32[]{:S(2)}, u32[]{:S(2)}) collective-permute-start(bf16[128,896]{1,0:T(8,128)(2,1)S(1)} %get-tuple-element.50.refs_3_.refs_1_), channel_id=1, source_target_pairs={{0,2},{1,3},{2,0},{3,1},{4,6},{5,7},{6,4},{7,5},{8,10},{9,11},{10,... | collective-permute-start | bytes 688136 | tf_op jit(solution)/shard_map/ppermute | solution.py:445
  25.0 14.0 %collective-permute-start.4 = (bf16[128,1024]{1,0:T(8,128)(2,1)S(1)}, bf16[128,1024]{1,0:T(8,128)(2,1)S(1)}, u32[]{:S(2)}, u32[]{:S(2)}) collective-permute-start(bf16[128,1024]{1,0:T(8,128)(2,1)S(1)} %smooth.6.s_ref), channel_id=1, source_target_pairs={{0,1},{1,0},{2,3},{3,2},{4,5},{5,4},{6,7},{7,6},{8,9},{9,8},{10,11... | collective-permute-start | bytes 786440 | tf_op jit(solution)/shard_map/ppermute | solution.py:499
  25.1 6.8 %collective-permute-start.5 = (bf16[144,128]{1,0:T(8,128)(2,1)S(1)}, bf16[144,128]{1,0:T(8,128)(2,1)S(1)}, u32[]{:S(2)}, u32[]{:S(2)}) collective-permute-start(bf16[144,128]{1,0:T(8,128)(2,1)S(1)} %get-tuple-element.40), channel_id=1, source_target_pairs={{0,1},{1,4},{4,5},{5,8},{8,9},{9,12},{12,13},{13,16},{16,17},{17,2... | collective-permute-start | bytes 110600 | tf_op jit(solution)/shard_map/ppermute | solution.py:480
  25.6 12.5 %collective-permute-start.9 = (bf16[128,640]{1,0:T(8,128)(2,1)S(1)}, bf16[128,640]{1,0:T(8,128)(2,1)S(1)}, u32[]{:S(2)}, u32[]{:S(2)}) collective-permute-start(bf16[128,640]{1,0:T(8,128)(2,1)S(1)} %get-tuple-element.48.refs_3_.refs_1_), channel_id=1, source_target_pairs={{0,2},{1,3},{2,0},{3,1},{4,6},{5,7},{6,4},{7,5},{8,10},{9,11},{10,... | collective-permute-start | bytes 491528 | tf_op jit(solution)/shard_map/ppermute | solution.py:445
  31.9 1.6 %collective-permute-start.6 = (bf16[144,128]{1,0:T(8,128)(2,1)S(1)}, bf16[144,128]{1,0:T(8,128)(2,1)S(1)}, u32[]{:S(2)}, u32[]{:S(2)}) collective-permute-start(bf16[144,128]{1,0:T(8,128)(2,1)S(1)} %get-tuple-element.41), channel_id=1, source_target_pairs={{1,0},{4,1},{5,4},{8,5},{9,8},{12,9},{13,12},{16,13},{17,16},{20,1... | collective-permute-start | bytes 110600 | tf_op jit(solution)/shard_map/ppermute | solution.py:481
  33.6 6.7 %collective-permute-start.8 = (bf16[128,512]{1,0:T(8,128)(2,1)S(1)}, bf16[128,512]{1,0:T(8,128)(2,1)S(1)}, u32[]{:S(2)}, u32[]{:S(2)}) collective-permute-start(bf16[128,512]{1,0:T(8,128)(2,1)S(1)} %get-tuple-element.47.refs_1_), channel_id=1, source_target_pairs={{0,2},{1,3},{2,0},{3,1},{4,6},{5,7},{6,4},{7,5},{8,10},{9,11},{10,... | collective-permute-start | bytes 393224 | tf_op jit(solution)/shard_map/ppermute | solution.py:445
  36.8 5.1 %collective-permute-start.13 = (bf16[128,896]{1,0:T(8,128)(2,1)S(1)}, bf16[128,896]{1,0:T(8,128)(2,1)S(1)}, u32[]{:S(2)}, u32[]{:S(2)}) collective-permute-start(bf16[128,896]{1,0:T(8,128)(2,1)S(1)} %smooth.9.s_ref), channel_id=1, source_target_pairs={{0,1},{1,0},{2,3},{3,2},{4,5},{5,4},{6,7},{7,6},{8,9},{9,8},{10,11... | collective-permute-start | bytes 688136 | tf_op jit(solution)/shard_map/ppermute | solution.py:499
  38.5 5.6 %collective-permute-start.12 = (bf16[128,640]{1,0:T(8,128)(2,1)S(1)}, bf16[128,640]{1,0:T(8,128)(2,1)S(1)}, u32[]{:S(2)}, u32[]{:S(2)}) collective-permute-start(bf16[128,640]{1,0:T(8,128)(2,1)S(1)} %smooth.8.s_ref), channel_id=1, source_target_pairs={{0,1},{1,0},{2,3},{3,2},{4,5},{5,4},{6,7},{7,6},{8,9},{9,8},{10,11... | collective-permute-start | bytes 491528 | tf_op jit(solution)/shard_map/ppermute | solution.py:499
  40.7 5.5 %collective-permute-start.10 = (bf16[128,640]{1,0:T(8,128)(2,1)S(1)}, bf16[128,640]{1,0:T(8,128)(2,1)S(1)}, u32[]{:S(2)}, u32[]{:S(2)}) collective-permute-start(bf16[128,640]{1,0:T(8,128)(2,1)S(1)} %smooth.7.s_ref), channel_id=1, source_target_pairs={{0,1},{1,0},{2,3},{3,2},{4,5},{5,4},{6,7},{7,6},{8,9},{9,8},{10,11... | collective-permute-start | bytes 491528 | tf_op jit(solution)/shard_map/ppermute | solution.py:499
where the time goes:
time: 47.5 us; the launch traced here: 47.2 us
  Pallas kernels  20.1 us (42%)
  waiting for transfers between devices  14.3 us (30%)
  starting transfers between devices  10.5 us (22%)
  local copies, waits for them, and re-layouts  2.19 us (5%)
    pallas_call x10, Pallas kernels, mix(): pl.pallas_call(body, out_shape=out, in_specs=specs, out_specs=out_specs,...  12 us
    ppermute x5, starting transfers between devices, sum_fields(): other = lax.ppermute(share, 'task', partners(size, bit))  8.46 us
    ppermute x5, waiting for transfers between devices, sum_fields(): other = lax.ppermute(share, 'task', partners(size, bit))  6.77 us
    ppermute x1, waiting for transfers between devices, steps_of(): from_left = lax.ppermute(right_edge, ('site', 'task'), up)  4.26 us
    pallas_call x2, Pallas kernels, project(): pl.pallas_call(body, out_shape=(shape((ranks, width), jnp.float32), shape...  3.88 us
    unnamed x6, local copies, waits for them, and re-layouts  2.19 us
    pallas_call x5, Pallas kernels, smooth(): pl.pallas_call(body, out_shape=shape((half, count), jnp.bfloat16), in_spe...  1.89 us
    ppermute x1, waiting for transfers between devices, steps_of(): from_right = lax.ppermute(left_edge, ('site', 'task'), down)  1.64 us
  transfers between devices with their start and end apart: 14, of which 5 were waited for; matrix products, arithmetic and copies ran while one was open for 0% of the time, Pallas kernels for 37%

commit v1 on v0

--- a/solution.py
+++ b/solution.py
@@ -15,7 +15,7 @@
 STEP = 512
 EDGE_ROWS = 16
 MIB = 1 << 20
-CUTS = (8, 16, 23, 28)
+CUTS = (9, 20, 27)
 
 VM = pl.BlockSpec(memory_space=pltpu.VMEM)
 HBM = pl.BlockSpec(memory_space=pltpu.HBM)
@@ -58,7 +58,7 @@
 def project(values, factors, groups, resident):
     tasks, ranks = factors.shape
     span, width = values.shape[1] // 2, len(groups) * GROUP
-    cuts = tiles(groups)
+    cuts = tiles(groups, 2 * STEP if resident else width)
 
     def body(f_hbm, v_hbm, own_ref, send_ref, v_ref, f_ref, sems):
         core = core_of()
@@ -484,7 +484,8 @@
     held_groups = chunks[:-1] + [chunks[-1] + [groups]]
 
     final = len(regions) - 1
-    parts = dict(zip(("mix0", "mix0b", "mix1", "mix1b"), regions[1:]))
+    middle = len(regions[1]) // 2
+    parts = {"mix0": regions[1][:middle], "mix0b": regions[1][middle:], "mix1": regions[2], "mix1b": regions[3]}
     kernels = [[] for _ in regions]
     kernels[0].append(kernel_blocks(tables, None, regions[0], groups))
 
@@ -502,7 +503,7 @@
             more = part and (tables, outside if part is regions[final] else None, part, groups)
             product, *built = mix(rows, factors, noise, values, product, region, mine, more)
             if built:
-                kernels[regions.index(part)].append(built[0])
+                kernels[1 if part[0] in regions[1] else regions.index(part)].append(built[0])
     return product
 
 

time: 47.5 us -> 45.8 us (0.964)
  Pallas kernels: 20.1 us -> 17.3 us
  waiting for transfers between devices: 14.3 us -> 15.3 us
    ppermute x5 -> x4, waiting for transfers between devices: 6.77 us -> 11.8 us  [sum_fields(): other = lax.ppermute(share, 'task', partners(size, bit))]
    ppermute x1, starting transfers between devices: 0.01 us -> 4.29 us  [steps_of(): from_right = lax.ppermute(left_edge, ('site', 'task'), down)]
    ppermute x5 -> x4, starting transfers between devices: 8.46 us -> 5.08 us  [sum_fields(): other = lax.ppermute(share, 'task', partners(size, bit))]
    ppermute x1, waiting for transfers between devices: 4.26 us -> 1.64 us  [steps_of(): from_left = lax.ppermute(right_edge, ('site', 'task'), up)]
    pallas_call x10 -> x8, Pallas kernels: 12 us -> 9.78 us  [mix(): pl.pallas_call(body, out_shape=out, in_specs=specs, out_specs=out_specs,...]
    ppermute x1, waiting for transfers between devices: 1.64 us -> 0.01 us  [steps_of(): from_right = lax.ppermute(left_edge, ('site', 'task'), down)]
    ppermute x5 -> x4, starting transfers between devices: 0.86 us -> 0.28 us  [steps_of(): other = lax.ppermute(smoothed, 'task', partners(peers, 1))]
    pallas_call x2, Pallas kernels: 3.88 us -> 3.33 us  [project(): pl.pallas_call(body, out_shape=(shape((ranks, width), jnp.float32), shape...]
  transfers between devices with their start and end apart: 14 -> 12, of which waited for: 5 -> 6; matrix products, arithmetic and copies ran while one was open for 0% -> 0% of each run, Pallas kernels for 37% -> 31%
where the time goes in v1:
time: 45.8 us; the launch traced here: 45.6 us
  Pallas kernels  17.3 us (38%)
  waiting for transfers between devices  15.3 us (33%)
  starting transfers between devices  10.5 us (23%)
  local copies, waits for them, and re-layouts  2.19 us (5%)
    ppermute x4, waiting for transfers between devices, sum_fields(): other = lax.ppermute(share, 'task', partners(size, bit))  11.8 us
    pallas_call x8, Pallas kernels, mix(): pl.pallas_call(body, out_shape=out, in_specs=specs, out_specs=out_specs,...  9.78 us
    ppermute x4, starting transfers between devices, sum_fields(): other = lax.ppermute(share, 'task', partners(size, bit))  5.08 us
    ppermute x1, starting transfers between devices, steps_of(): from_right = lax.ppermute(left_edge, ('site', 'task'), down)  4.29 us
    pallas_call x2, Pallas kernels, project(): pl.pallas_call(body, out_shape=(shape((ranks, width), jnp.float32), shape...  3.33 us
    unnamed x6, local copies, waits for them, and re-layouts  2.19 us
    pallas_call x4, Pallas kernels, smooth(): pl.pallas_call(body, out_shape=shape((half, count), jnp.bfloat16), in_spe...  1.74 us
    ppermute x1, waiting for transfers between devices, steps_of(): from_left = lax.ppermute(right_edge, ('site', 'task'), up)  1.64 us
  transfers between devices with their start and end apart: 12, of which 6 were waited for; matrix products, arithmetic and copies ran while one was open for 0% of the time, Pallas kernels for 31%

profile of v1, /device:TPU:0, one launch (start us, length us, event | category | flops | bytes accessed | tf_op | source)
XLA Modules:
  0.0 45.6 jit_solution(11474756346501236759)
XLA Ops:
  0.0 2.2 %copy-done = bf16[256,8192]{1,0:T(8,128)(2,1)S(1)} copy-done((bf16[256,8192]{1,0:T(8,128)(2,1)S(1)}, bf16[256,8192]{1,0:T(8,128)(2,1)}, u32[]{:S(2)}) %copy-start) | copy-done | bytes 4194328
  2.2 1.6 %project.3 = (f32[128,2816]{1,0:T(8,128)S(1)}, bf16[128,2816]{1,0:T(8,128)(2,1)S(1)}) custom-call(bf16[256,128]{1,0:T(8,128)(2,1)} %f_ref.15, bf16[256,8192]{1,0:T(8,128)(2,1)S(1)} %copy-done), custom_call_target="tpu_custom_call" | custom-call | flops 369098752 | bytes 2883584 | tf_op jit(solution)/shard_map/project/pallas_call | solution.py:85
  3.8 0.6 %collective-permute-start.3 = (bf16[128,2816]{1,0:T(8,128)(2,1)S(1)}, bf16[128,2816]{1,0:T(8,128)(2,1)S(1)}, u32[]{:S(2)}, u32[]{:S(2)}) collective-permute-start(bf16[128,2816]{1,0:T(8,128)(2,1)S(1)} %get-tuple-element.38), channel_id=1, source_target_pairs={{0,1},{1,0},{2,3},{3,2},{4,5},{5,4},{6,7},{7,6},{8,9},{9,8},{10,11... | collective-permute-start | bytes 2162696 | tf_op jit(solution)/shard_map/ppermute | solution.py:472
  4.4 1.7 %project.2 = (f32[128,1280]{1,0:T(8,128)S(1)}, bf16[128,1280]{1,0:T(8,128)(2,1)S(1)}) custom-call(bf16[256,128]{1,0:T(8,128)(2,1)} %f_ref.15, bf16[256,8192]{1,0:T(8,128)(2,1)} %v_ref.15), custom_call_target="tpu_custom_call" | custom-call | flops 167772160 | bytes 1310720 | tf_op jit(solution)/shard_map/project/pallas_call | solution.py:85
  6.2 1.6 %collective-permute-done.got_ref = bf16[128,1280]{1,0:T(8,128)(2,1)S(1)} collective-permute-done((bf16[128,1280]{1,0:T(8,128)(2,1)S(1)}, bf16[128,1280]{1,0:T(8,128)(2,1)S(1)}, u32[]{:S(2)}, u32[]{:S(2)}) %collective-permute-start) | collective-permute-done | bytes 327712 | tf_op jit(solution)/shard_map/ppermute | solution.py:467
  7.9 2.7 %collective-permute-start.1 = (bf16[128,1280]{1,0:T(8,128)(2,1)S(1)}, bf16[128,1280]{1,0:T(8,128)(2,1)S(1)}, u32[]{:S(2)}, u32[]{:S(2)}) collective-permute-start(bf16[128,1280]{1,0:T(8,128)(2,1)S(1)} %add_cores.2.refs_1_.refs_4_.first_ref.refs_5_), channel_id=1, source_target_pairs={{0,2},{1,3},{2,0},{3,1},{4,6},{5,7},{6,4},{7,5},{8,10},{9,11},{10,... | collective-permute-start | bytes 983048 | tf_op jit(solution)/shard_map/ppermute | solution.py:445
  10.8 1.0 %make_tables.1 = (bf16[2,4096]{1,0:T(2,128)(2,1)S(1)}, f32[2,16,128]{2,1,0:T(8,128)S(1)}, f32[32,128]{1,0:T(8,128)S(1)}, f32[256,128]{1,0:T(8,128)S(1)}) custom-call(bf16[2,8192]{1,0:T(2,128)(2,1)} %j_hbm.1, s32[3,32]{1,0:T(4,128)} %bitcast.3, f32[1,4]{1,0:T(1,128)} %bitcast.5, f32[1,256]{1,0:T(1,128)} %bitcast.4), custom_call_target="tpu_custom_call" | custom-call | flops 16384 | bytes 65536 | tf_op jit(solution)/shard_map/make_tables/pallas_call | solution.py:133
  11.8 1.2 %kernel_blocks.1.refs_0_ = bf16[8,256,512]{2,1,0:T(8,128)(2,1)S(1)} custom-call(bf16[2,4096]{1,0:T(2,128)(2,1)S(1)} %get-tuple-element.28.refs_0_.rest_0_.j_ref, f32[2,16,128]{2,1,0:T(8,128)S(1)} %get-tuple-element.29.refs_1_.rest_1_, f32[32,128]{1,0:T(8,128)S(1)} %get-tuple-element.30.refs_2_.rest_2_), custom_call_target="tpu_custom_call" | custom-call | flops 31457280 | bytes 2097152 | tf_op jit(solution)/shard_map/kernel_blocks/pallas_call | solution.py:312
  13.0 6.1 %collective-permute-done.1.refs_2_.refs_5_.refs_6_ = bf16[128,1280]{1,0:T(8,128)(2,1)S(1)} collective-permute-done((bf16[128,1280]{1,0:T(8,128)(2,1)S(1)}, bf16[128,1280]{1,0:T(8,128)(2,1)S(1)}, u32[]{:S(2)}, u32[]{:S(2)}) %collective-permute-start.1) | collective-permute-done | bytes 327712 | tf_op jit(solution)/shard_map/ppermute | solution.py:445
  19.7 1.2 %mix.8 = (f32[256,8192]{1,0:T(8,128)}, bf16[5,256,512]{2,1,0:T(8,128)(2,1)S(1)}) custom-call(bf16[128,1024]{1,0:T(8,128)(2,1)S(1)} %smooth.4.s_ref, bf16[256,128]{1,0:T(8,128)(2,1)S(1)} %copy-done.2, f32[256,128]{1,0:T(8,128)S(1)} %get-tuple-element.33.g_ref, bf16[256,8192]{1,0:T(8,128)(2,1)S(1)} %copy-done.1, ...), custom_call_target="tpu_custom_call" | custom-call | flops 86769664 | bytes 2359296 | tf_op jit(solution)/shard_map/mix/pallas_call | solution.py:413
  21.2 1.2 %mix.9 = (f32[256,8192]{1,0:T(8,128)}, bf16[6,256,512]{2,1,0:T(8,128)(2,1)S(1)}) custom-call(bf16[128,1024]{1,0:T(8,128)(2,1)S(1)} %collective-permute-done.2.s_ref, bf16[256,128]{1,0:T(8,128)(2,1)S(1)} %copy-done.2, f32[256,128]{1,0:T(8,128)S(1)} %get-tuple-element.33.g_ref, bf16[256,8192]{1,0:T(8,128)(2,1)S(1)} %copy-done.1, ...), custom_call_target="tpu_custom_call", output_to_operand_aliasing={{0}: (7, {})} | custom-call | flops 90701824 | bytes 2621440 | tf_op jit(solution)/shard_map/mix/pallas_call | solution.py:413
  22.4 4.1 %collective-permute-done.4.refs_3_.refs_4_ = bf16[128,1408]{1,0:T(8,128)(2,1)S(1)} collective-permute-done((bf16[128,1408]{1,0:T(8,128)(2,1)S(1)}, bf16[128,1408]{1,0:T(8,128)(2,1)S(1)}, u32[]{:S(2)}, u32[]{:S(2)}) %collective-permute-start.4) | collective-permute-done | bytes 360480 | tf_op jit(solution)/shard_map/ppermute | solution.py:445
  26.5 0.5 %smooth.5.s_ref = bf16[128,1408]{1,0:T(8,128)(2,1)S(1)} custom-call(bf16[5,256,512]{2,1,0:T(8,128)(2,1)S(1)} %get-tuple-element.34.refs_0_, bf16[6,256,512]{2,1,0:T(8,128)(2,1)S(1)} %get-tuple-element.36.refs_1_, bf16[128,1408]{1,0:T(8,128)(2,1)S(1)} %get-tuple-element.39.refs_2_.refs_3_, bf16[128,1408]{1,0:T(8,128)(2,1)S(1)} %collective-permute-done.4.refs_3_.refs_4_, ...), custom_call_target="tpu_custom_call" | custom-call | flops 184549376 | bytes 2883584 | tf_op jit(solution)/shard_map/smooth/pallas_call | solution.py:366
  27.1 1.8 %collective-permute-start.9 = (bf16[128,896]{1,0:T(8,128)(2,1)S(1)}, bf16[128,896]{1,0:T(8,128)(2,1)S(1)}, u32[]{:S(2)}, u32[]{:S(2)}) collective-permute-start(bf16[128,896]{1,0:T(8,128)(2,1)S(1)} %get-tuple-element.48.refs_3_.refs_1_), channel_id=1, source_target_pairs={{0,2},{1,3},{2,0},{3,1},{4,6},{5,7},{6,4},{7,5},{8,10},{9,11},{10,... | collective-permute-start | bytes 688136 | tf_op jit(solution)/shard_map/ppermute | solution.py:445
  29.2 4.3 %collective-permute-start.7 = (bf16[144,128]{1,0:T(8,128)(2,1)S(1)}, bf16[144,128]{1,0:T(8,128)(2,1)S(1)}, u32[]{:S(2)}, u32[]{:S(2)}) collective-permute-start(bf16[144,128]{1,0:T(8,128)(2,1)S(1)} %get-tuple-element.42), channel_id=1, source_target_pairs={{1,0},{4,1},{5,4},{8,5},{9,8},{12,9},{13,12},{16,13},{17,16},{20,1... | collective-permute-start | bytes 110600 | tf_op jit(solution)/shard_map/ppermute | solution.py:481
  33.5 1.6 %collective-permute-done.6.left_ref = bf16[144,128]{1,0:T(8,128)(2,1)S(1)} collective-permute-done((bf16[144,128]{1,0:T(8,128)(2,1)S(1)}, bf16[144,128]{1,0:T(8,128)(2,1)S(1)}, u32[]{:S(2)}, u32[]{:S(2)}) %collective-permute-start.6) | collective-permute-done | bytes 36896 | tf_op jit(solution)/shard_map/ppermute | solution.py:480
  35.1 0.5 %collective-permute-start.8 = (bf16[128,640]{1,0:T(8,128)(2,1)S(1)}, bf16[128,640]{1,0:T(8,128)(2,1)S(1)}, u32[]{:S(2)}, u32[]{:S(2)}) collective-permute-start(bf16[128,640]{1,0:T(8,128)(2,1)S(1)} %get-tuple-element.47.refs_1_), channel_id=1, source_target_pairs={{0,2},{1,3},{2,0},{3,1},{4,6},{5,7},{6,4},{7,5},{8,10},{9,11},{10,... | collective-permute-start | bytes 491528 | tf_op jit(solution)/shard_map/ppermute | solution.py:445
  35.6 1.4 %mix.10 = (f32[256,8192]{1,0:T(8,128)}, bf16[7,256,512]{2,1,0:T(8,128)(2,1)S(1)}) custom-call(bf16[128,1408]{1,0:T(8,128)(2,1)S(1)} %smooth.5.s_ref, bf16[256,128]{1,0:T(8,128)(2,1)S(1)} %copy-done.2, f32[256,128]{1,0:T(8,128)S(1)} %get-tuple-element.33.g_ref, bf16[256,8192]{1,0:T(8,128)(2,1)S(1)} %copy-done.1, ...), custom_call_target="tpu_custom_call", output_to_operand_aliasing={{0}: (7, {})} | custom-call | flops 119799808 | bytes 3276800 | tf_op jit(solution)/shard_map/mix/pallas_call | solution.py:413
  37.5 1.4 %mix.11 = (f32[256,8192]{1,0:T(8,128)}, bf16[6,256,512]{2,1,0:T(8,128)(2,1)S(1)}) custom-call(bf16[128,1408]{1,0:T(8,128)(2,1)S(1)} %collective-permute-done.5.s_ref, bf16[256,128]{1,0:T(8,128)(2,1)S(1)} %copy-done.2, f32[256,128]{1,0:T(8,128)S(1)} %get-tuple-element.33.g_ref, bf16[256,8192]{1,0:T(8,128)(2,1)S(1)} %copy-done.1, ...), custom_call_target="tpu_custom_call", output_to_operand_aliasing={{0}: (8, {})} | custom-call | flops 115867648 | bytes 3014656 | tf_op jit(solution)/shard_map/mix/pallas_call | solution.py:413
  38.9 1.6 %collective-permute-done.8.refs_2_ = bf16[128,640]{1,0:T(8,128)(2,1)S(1)} collective-permute-done((bf16[128,640]{1,0:T(8,128)(2,1)S(1)}, bf16[128,640]{1,0:T(8,128)(2,1)S(1)}, u32[]{:S(2)}, u32[]{:S(2)}) %collective-permute-start.8) | collective-permute-done | bytes 163872 | tf_op jit(solution)/shard_map/ppermute | solution.py:445
  41.0 1.2 %mix.12.rest_0_ = f32[256,8192]{1,0:T(8,128)} custom-call(bf16[128,896]{1,0:T(8,128)(2,1)S(1)} %smooth.7.s_ref, bf16[256,128]{1,0:T(8,128)(2,1)S(1)} %copy-done.2, f32[256,128]{1,0:T(8,128)S(1)} %get-tuple-element.33.g_ref, bf16[256,8192]{1,0:T(8,128)(2,1)S(1)} %copy-done.1, f32[256,8192]{1,0:T(8,128)} %get-tuple-element.50.rest_0_), custom_call_target="tpu_custom_call", output_to_operand_aliasing={{}: (4, {})} | custom-call | flops 58720256 | bytes 917504 | tf_op jit(solution)/shard_map/mix/pallas_call | solution.py:413
  42.2 1.2 %mix.13.rest_0_ = f32[256,8192]{1,0:T(8,128)} custom-call(bf16[128,896]{1,0:T(8,128)(2,1)S(1)} %collective-permute-done.11.s_ref, bf16[256,128]{1,0:T(8,128)(2,1)S(1)} %copy-done.2, f32[256,128]{1,0:T(8,128)S(1)} %get-tuple-element.33.g_ref, bf16[256,8192]{1,0:T(8,128)(2,1)S(1)} %copy-done.1, f32[256,8192]{1,0:T(8,128)} %mix.12.rest_0_), custom_call_target="tpu_custom_call", output_to_operand_aliasing={{}: (4, {})} | custom-call | flops 58720256 | bytes 917504 | tf_op jit(solution)/shard_map/mix/pallas_call | solution.py:413
  43.3 1.1 %mix.14.rest_0_ = f32[256,8192]{1,0:T(8,128)} custom-call(bf16[128,768]{1,0:T(8,128)(2,1)S(1)} %smooth.6.s_ref, bf16[256,128]{1,0:T(8,128)(2,1)S(1)} %copy-done.2, f32[256,128]{1,0:T(8,128)S(1)} %get-tuple-element.33.g_ref, bf16[256,8192]{1,0:T(8,128)(2,1)S(1)} %copy-done.1, f32[256,8192]{1,0:T(8,128)} %mix.13.rest_0_), custom_call_target="tpu_custom_call", output_to_operand_aliasing={{}: (4, {})} | custom-call | flops 50331648 | bytes 786432 | tf_op jit(solution)/shard_map/mix/pallas_call | solution.py:413
  44.4 1.1 %mix.15 = f32[256,8192]{1,0:T(8,128)} custom-call(bf16[128,768]{1,0:T(8,128)(2,1)S(1)} %collective-permute-done.10.s_ref, bf16[256,128]{1,0:T(8,128)(2,1)S(1)} %copy-done.2, f32[256,128]{1,0:T(8,128)S(1)} %get-tuple-element.33.g_ref, bf16[256,8192]{1,0:T(8,128)(2,1)S(1)} %copy-done.1, f32[256,8192]{1,0:T(8,128)} %mix.14.rest_0_), custom_call_target="tpu_custom_call", output_to_operand_aliasing={{}: (4, {})} | custom-call | flops 50331648 | bytes 786432 | tf_op jit(solution)/shard_map/mix/pallas_call | solution.py:413
  (26 shorter events, 2.4 us)
Async XLA Ops:
  0.0 2.2 %copy-start = (bf16[256,8192]{1,0:T(8,128)(2,1)S(1)}, bf16[256,8192]{1,0:T(8,128)(2,1)}, u32[]{:S(2)}) copy-start(bf16[256,8192]{1,0:T(8,128)(2,1)} %v_ref.15) | copy-start | bytes 12582916
  2.2 17.5 %copy-start.1 = (bf16[256,8192]{1,0:T(8,128)(2,1)S(1)}, bf16[256,8192]{1,0:T(8,128)(2,1)}, u32[]{:S(2)}) copy-start(bf16[256,8192]{1,0:T(8,128)(2,1)} %v_ref.15) | copy-start | bytes 12582916
  2.2 17.5 %copy-start.2 = (bf16[256,128]{1,0:T(8,128)(2,1)S(1)}, bf16[256,128]{1,0:T(8,128)(2,1)}, u32[]{:S(2)}) copy-start(bf16[256,128]{1,0:T(8,128)(2,1)} %f_ref.15) | copy-start | bytes 196612
  3.8 6.7 %collective-permute-start.3 = (bf16[128,2816]{1,0:T(8,128)(2,1)S(1)}, bf16[128,2816]{1,0:T(8,128)(2,1)S(1)}, u32[]{:S(2)}, u32[]{:S(2)}) collective-permute-start(bf16[128,2816]{1,0:T(8,128)(2,1)S(1)} %get-tuple-element.38), channel_id=1, source_target_pairs={{0,1},{1,0},{2,3},{3,2},{4,5},{5,4},{6,7},{7,6},{8,9},{9,8},{10,11... | collective-permute-start | bytes 2162696 | tf_op jit(solution)/shard_map/ppermute | solution.py:472
  6.1 1.7 %collective-permute-start = (bf16[128,1280]{1,0:T(8,128)(2,1)S(1)}, bf16[128,1280]{1,0:T(8,128)(2,1)S(1)}, u32[]{:S(2)}, u32[]{:S(2)}) collective-permute-start(bf16[128,1280]{1,0:T(8,128)(2,1)S(1)} %get-tuple-element.32), channel_id=1, source_target_pairs={{0,1},{1,0},{2,3},{3,2},{4,5},{5,4},{6,7},{7,6},{8,9},{9,8},{10,11... | collective-permute-start | bytes 983048 | tf_op jit(solution)/shard_map/ppermute | solution.py:467
  7.9 11.3 %collective-permute-start.1 = (bf16[128,1280]{1,0:T(8,128)(2,1)S(1)}, bf16[128,1280]{1,0:T(8,128)(2,1)S(1)}, u32[]{:S(2)}, u32[]{:S(2)}) collective-permute-start(bf16[128,1280]{1,0:T(8,128)(2,1)S(1)} %add_cores.2.refs_1_.refs_4_.first_ref.refs_5_), channel_id=1, source_target_pairs={{0,2},{1,3},{2,0},{3,1},{4,6},{5,7},{6,4},{7,5},{8,10},{9,11},{10,... | collective-permute-start | bytes 983048 | tf_op jit(solution)/shard_map/ppermute | solution.py:445
  10.7 15.8 %collective-permute-start.4 = (bf16[128,1408]{1,0:T(8,128)(2,1)S(1)}, bf16[128,1408]{1,0:T(8,128)(2,1)S(1)}, u32[]{:S(2)}, u32[]{:S(2)}) collective-permute-start(bf16[128,1408]{1,0:T(8,128)(2,1)S(1)} %get-tuple-element.39.refs_2_.refs_3_), channel_id=1, source_target_pairs={{0,2},{1,3},{2,0},{3,1},{4,6},{5,7},{6,4},{7,5},{8,10},{9,11},{10,... | collective-permute-start | bytes 1081352 | tf_op jit(solution)/shard_map/ppermute | solution.py:445
  19.6 1.6 %collective-permute-start.2 = (bf16[128,1024]{1,0:T(8,128)(2,1)S(1)}, bf16[128,1024]{1,0:T(8,128)(2,1)S(1)}, u32[]{:S(2)}, u32[]{:S(2)}) collective-permute-start(bf16[128,1024]{1,0:T(8,128)(2,1)S(1)} %smooth.4.s_ref), channel_id=1, source_target_pairs={{0,1},{1,0},{2,3},{3,2},{4,5},{5,4},{6,7},{7,6},{8,9},{9,8},{10,11... | collective-permute-start | bytes 786440 | tf_op jit(solution)/shard_map/ppermute | solution.py:500
  27.1 10.4 %collective-permute-start.5 = (bf16[128,1408]{1,0:T(8,128)(2,1)S(1)}, bf16[128,1408]{1,0:T(8,128)(2,1)S(1)}, u32[]{:S(2)}, u32[]{:S(2)}) collective-permute-start(bf16[128,1408]{1,0:T(8,128)(2,1)S(1)} %smooth.5.s_ref), channel_id=1, source_target_pairs={{0,1},{1,0},{2,3},{3,2},{4,5},{5,4},{6,7},{7,6},{8,9},{9,8},{10,11... | collective-permute-start | bytes 1081352 | tf_op jit(solution)/shard_map/ppermute | solution.py:500
  27.1 9.9 %collective-permute-start.9 = (bf16[128,896]{1,0:T(8,128)(2,1)S(1)}, bf16[128,896]{1,0:T(8,128)(2,1)S(1)}, u32[]{:S(2)}, u32[]{:S(2)}) collective-permute-start(bf16[128,896]{1,0:T(8,128)(2,1)S(1)} %get-tuple-element.48.refs_3_.refs_1_), channel_id=1, source_target_pairs={{0,2},{1,3},{2,0},{3,1},{4,6},{5,7},{6,4},{7,5},{8,10},{9,11},{10,... | collective-permute-start | bytes 688136 | tf_op jit(solution)/shard_map/ppermute | solution.py:445
  29.0 6.1 %collective-permute-start.6 = (bf16[144,128]{1,0:T(8,128)(2,1)S(1)}, bf16[144,128]{1,0:T(8,128)(2,1)S(1)}, u32[]{:S(2)}, u32[]{:S(2)}) collective-permute-start(bf16[144,128]{1,0:T(8,128)(2,1)S(1)} %get-tuple-element.41), channel_id=1, source_target_pairs={{0,1},{1,4},{4,5},{5,8},{8,9},{9,12},{12,13},{13,16},{16,17},{17,2... | collective-permute-start | bytes 110600 | tf_op jit(solution)/shard_map/ppermute | solution.py:480
  29.2 5.9 %collective-permute-start.7 = (bf16[144,128]{1,0:T(8,128)(2,1)S(1)}, bf16[144,128]{1,0:T(8,128)(2,1)S(1)}, u32[]{:S(2)}, u32[]{:S(2)}) collective-permute-start(bf16[144,128]{1,0:T(8,128)(2,1)S(1)} %get-tuple-element.42), channel_id=1, source_target_pairs={{1,0},{4,1},{5,4},{8,5},{9,8},{12,9},{13,12},{16,13},{17,16},{20,1... | collective-permute-start | bytes 110600 | tf_op jit(solution)/shard_map/ppermute | solution.py:481
  35.1 5.4 %collective-permute-start.8 = (bf16[128,640]{1,0:T(8,128)(2,1)S(1)}, bf16[128,640]{1,0:T(8,128)(2,1)S(1)}, u32[]{:S(2)}, u32[]{:S(2)}) collective-permute-start(bf16[128,640]{1,0:T(8,128)(2,1)S(1)} %get-tuple-element.47.refs_1_), channel_id=1, source_target_pairs={{0,2},{1,3},{2,0},{3,1},{4,6},{5,7},{6,4},{7,5},{8,10},{9,11},{10,... | collective-permute-start | bytes 491528 | tf_op jit(solution)/shard_map/ppermute | solution.py:445
  37.4 4.7 %collective-permute-start.11 = (bf16[128,896]{1,0:T(8,128)(2,1)S(1)}, bf16[128,896]{1,0:T(8,128)(2,1)S(1)}, u32[]{:S(2)}, u32[]{:S(2)}) collective-permute-start(bf16[128,896]{1,0:T(8,128)(2,1)S(1)} %smooth.7.s_ref), channel_id=1, source_target_pairs={{0,1},{1,0},{2,3},{3,2},{4,5},{5,4},{6,7},{7,6},{8,9},{9,8},{10,11... | collective-permute-start | bytes 688136 | tf_op jit(solution)/shard_map/ppermute | solution.py:500
  40.9 3.5 %collective-permute-start.10 = (bf16[128,768]{1,0:T(8,128)(2,1)S(1)}, bf16[128,768]{1,0:T(8,128)(2,1)S(1)}, u32[]{:S(2)}, u32[]{:S(2)}) collective-permute-start(bf16[128,768]{1,0:T(8,128)(2,1)S(1)} %smooth.6.s_ref), channel_id=1, source_target_pairs={{0,1},{1,0},{2,3},{3,2},{4,5},{5,4},{6,7},{7,6},{8,9},{9,8},{10,11... | collective-permute-start | bytes 589832 | tf_op jit(solution)/shard_map/ppermute | solution.py:500

commit v2 on v1

--- a/solution.py
+++ b/solution.py
@@ -15,7 +15,7 @@
 STEP = 512
 EDGE_ROWS = 16
 MIB = 1 << 20
-CUTS = (9, 20, 27)
+CUTS = (7, 20, 27)
 
 VM = pl.BlockSpec(memory_space=pltpu.VMEM)
 HBM = pl.BlockSpec(memory_space=pltpu.HBM)
@@ -55,45 +55,46 @@
     return pl.ds(pl.multiple_of(side * span + begin, GROUP), size)
 
 
-def project(values, factors, groups, resident):
+def project(values, factors, groups, resident, mine):
     tasks, ranks = factors.shape
     span, width = values.shape[1] // 2, len(groups) * GROUP
     cuts = tiles(groups, 2 * STEP if resident else width)
 
-    def body(f_hbm, v_hbm, own_ref, send_ref, v_ref, f_ref, sems):
-        core = core_of()
-        first = pltpu.make_async_copy(f_hbm, f_ref, sems.at[2 * len(cuts)])
+    kind = jnp.float32 if mine else jnp.bfloat16
+
+    def body(f_hbm, v_hbm, out, v_ref, f_ref, sems):
+        side = core_of() if mine else 1 - core_of()
+        first = pltpu.make_async_copy(f_hbm, f_ref, sems.at[len(cuts)])
         first.start()
-        work = [(send_ref, 1 - core, *cut) for cut in cuts] + [(own_ref, core, *cut) for cut in cuts]
         copies = [] if resident else [
-            pltpu.make_async_copy(v_hbm.at[:, columns(at, size, side, span)], v_ref.at[i // len(cuts), :, pl.ds(place, size)], sems.at[i])
-            for i, (_, side, at, place, size) in enumerate(work)
+            pltpu.make_async_copy(v_hbm.at[:, columns(at, size, side, span)], v_ref.at[:, pl.ds(place, size)], sems.at[i])
+            for i, (at, place, size) in enumerate(cuts)
         ]
         for copy in copies:
             copy.start()
         first.wait()
         turned = f_ref[...].astype(jnp.float32).T.astype(jnp.bfloat16)
-        for i, (out, side, at, place, size) in enumerate(work):
+        for i, (at, place, size) in enumerate(cuts):
             s = slice(place, place + size)
             if resident:
                 field = v_hbm[:, columns(at, size, side, span)]
             else:
                 copies[i].wait()
-                field = v_ref[i // len(cuts), :, s]
-            out[:, s] = jnp.dot(turned, field, preferred_element_type=jnp.float32).astype(out.dtype)
-
-    return pl.pallas_call(
-        body,
-        out_shape=(shape((ranks, width), jnp.float32), shape((ranks, width), jnp.bfloat16)),
+                field = v_ref[:, s]
+            out[:, s] = jnp.dot(turned, field, preferred_element_type=jnp.float32).astype(kind)
+
+    return pl.pallas_call(
+        body,
+        out_shape=shape((ranks, width), kind),
         in_specs=[HBM, VM if resident else HBM],
-        out_specs=(VM, VM),
+        out_specs=VM,
         scratch_shapes=[
-            pltpu.VMEM((1, 16, GROUP) if resident else (2, tasks, width), values.dtype),
+            pltpu.VMEM((16, GROUP) if resident else (tasks, width), values.dtype),
             pltpu.VMEM(factors.shape, factors.dtype),
-            pltpu.SemaphoreType.DMA((2 * len(cuts) + 1,)),
+            pltpu.SemaphoreType.DMA((len(cuts) + 1,)),
         ],
         compiler_params=grant(14),
-        cost_estimate=cost(4 * tasks * ranks * width, tasks * width * 4),
+        cost_estimate=cost(2 * tasks * ranks * width, tasks * width * 2),
         name="project",
     )(in_hbm(factors), values if resident else in_hbm(values))
 
@@ -463,14 +464,16 @@
     groups = values.shape[1] // (2 * GROUP)
     regions, chunks = plan(groups)
     rest = [g for chunk in chunks[1:] for g in chunk]
-    own, send = project(values, factors, chunks[0], False)
+    send = project(values, factors, chunks[0], False, False)
     received = lax.ppermute(send, "task", partners(peers, 1))
+    own = project(values, factors, chunks[0], False, True)
     *tables, noise = make_tables(jitter, neighbours.T, length_scales.reshape(1, -1), nugget.reshape(1, -1))
     (share,) = add_cores(own, received, chunks[0], chunks[:1])
     sums = [sum_fields(share, peers)]
-    own, send = project(values, factors, rest, True)
+    send = project(values, factors, rest, True, False)
+    own_rest = project(values, factors, rest, True, True)
     received = lax.ppermute(send, "task", partners(peers, 1))
-    shares = add_cores(own, received, rest, chunks[1:])
+    shares = add_cores(own_rest, received, rest, chunks[1:])
     for part in shares[:-1]:
         sums.append(sum_fields(part, peers))
     left_edge, right_edge = take_edges(share, shares[-1], tables[0])

time: 45.8 us -> 45.2 us (0.987)
  waiting for transfers between devices: 15.3 us -> 12.6 us
  Pallas kernels: 17.3 us -> 19.2 us
    pallas_call x2 -> x4, Pallas kernels: 3.33 us -> 5.4 us  [project(): pl.pallas_call(body, out_shape=shape((ranks, width), kind), in_specs=[HBM...]
    ppermute x2, waiting for transfers between devices: 1.61 us -> 0.18 us  [steps_of(): received = lax.ppermute(send, 'task', partners(peers, 1))]
    ppermute x4, waiting for transfers between devices: 11.8 us -> 10.5 us  [sum_fields(): other = lax.ppermute(share, 'task', partners(size, bit))]
  transfers between devices with their start and end apart: 12 -> 12, of which waited for: 6 -> 6; matrix products, arithmetic and copies ran while one was open for 0% -> 0% of each run, Pallas kernels for 31% -> 36%
where the time goes in v2:
time: 45.2 us; the launch traced here: 45 us
  Pallas kernels  19.2 us (42%)
  waiting for transfers between devices  12.6 us (28%)
  starting transfers between devices  10.7 us (24%)
  local copies, waits for them, and re-layouts  2.2 us (5%)
    ppermute x4, waiting for transfers between devices, sum_fields(): other = lax.ppermute(share, 'task', partners(size, bit))  10.5 us
    pallas_call x8, Pallas kernels, mix(): pl.pallas_call(body, out_shape=out, in_specs=specs, out_specs=out_specs,...  9.86 us
    pallas_call x4, Pallas kernels, project(): pl.pallas_call(body, out_shape=shape((ranks, width), kind), in_specs=[HBM...  5.4 us
    ppermute x4, starting transfers between devices, sum_fields(): other = lax.ppermute(share, 'task', partners(size, bit))  5.27 us
    ppermute x1, starting transfers between devices, steps_of(): from_right = lax.ppermute(left_edge, ('site', 'task'), down)  4.29 us
    unnamed x6, local copies, waits for them, and re-layouts  2.2 us
    pallas_call x4, Pallas kernels, smooth(): pl.pallas_call(body, out_shape=shape((half, count), jnp.bfloat16), in_spe...  1.72 us
    ppermute x1, waiting for transfers between devices, steps_of(): from_left = lax.ppermute(right_edge, ('site', 'task'), up)  1.64 us
  transfers between devices with their start and end apart: 12, of which 6 were waited for; matrix products, arithmetic and copies ran while one was open for 0% of the time, Pallas kernels for 36%

profile of v2, /device:TPU:0, one launch (start us, length us, event | category | flops | bytes accessed | tf_op | source)
XLA Modules:
  0.0 45.0 jit_solution(12975030494635435756)
XLA Ops:
  0.0 2.2 %copy-done = bf16[256,8192]{1,0:T(8,128)(2,1)S(1)} copy-done((bf16[256,8192]{1,0:T(8,128)(2,1)S(1)}, bf16[256,8192]{1,0:T(8,128)(2,1)}, u32[]{:S(2)}) %copy-start) | copy-done | bytes 4194328
  2.2 1.4 %project.7 = bf16[128,3072]{1,0:T(8,128)(2,1)S(1)} custom-call(bf16[256,128]{1,0:T(8,128)(2,1)} %f_ref.15, bf16[256,8192]{1,0:T(8,128)(2,1)S(1)} %copy-done), custom_call_target="tpu_custom_call" | custom-call | flops 201326592 | bytes 1572864 | tf_op jit(solution)/shard_map/project/pallas_call | solution.py:86
  3.6 0.6 %collective-permute-start.3 = (bf16[128,3072]{1,0:T(8,128)(2,1)S(1)}, bf16[128,3072]{1,0:T(8,128)(2,1)S(1)}, u32[]{:S(2)}, u32[]{:S(2)}) collective-permute-start(bf16[128,3072]{1,0:T(8,128)(2,1)S(1)} %project.7), channel_id=1, source_target_pairs={{0,1},{1,0},{2,3},{3,2},{4,5},{5,4},{6,7},{7,6},{8,9},{9,8},{10,11... | collective-permute-start | bytes 2359304 | tf_op jit(solution)/shard_map/ppermute | solution.py:475
  4.2 1.3 %project.5 = bf16[128,1024]{1,0:T(8,128)(2,1)S(1)} custom-call(bf16[256,128]{1,0:T(8,128)(2,1)} %f_ref.15, bf16[256,8192]{1,0:T(8,128)(2,1)} %v_ref.15), custom_call_target="tpu_custom_call" | custom-call | flops 67108864 | bytes 524288 | tf_op jit(solution)/shard_map/project/pallas_call | solution.py:86
  5.6 1.3 %project.4.own_ref = f32[128,1024]{1,0:T(8,128)S(1)} custom-call(bf16[256,128]{1,0:T(8,128)(2,1)} %f_ref.15, bf16[256,8192]{1,0:T(8,128)(2,1)} %v_ref.15), custom_call_target="tpu_custom_call" | custom-call | flops 67108864 | bytes 524288 | tf_op jit(solution)/shard_map/project/pallas_call | solution.py:86
  7.2 2.9 %collective-permute-start.1 = (bf16[128,1024]{1,0:T(8,128)(2,1)S(1)}, bf16[128,1024]{1,0:T(8,128)(2,1)S(1)}, u32[]{:S(2)}, u32[]{:S(2)}) collective-permute-start(bf16[128,1024]{1,0:T(8,128)(2,1)S(1)} %add_cores.2.refs_1_.refs_4_.first_ref.refs_5_), channel_id=1, source_target_pairs={{0,2},{1,3},{2,0},{3,1},{4,6},{5,7},{6,4},{7,5},{8,10},{9,11},{10,... | collective-permute-start | bytes 786440 | tf_op jit(solution)/shard_map/ppermute | solution.py:446
  10.1 1.3 %project.6.own_ref = f32[128,3072]{1,0:T(8,128)S(1)} custom-call(bf16[256,128]{1,0:T(8,128)(2,1)} %f_ref.15, bf16[256,8192]{1,0:T(8,128)(2,1)S(1)} %copy-done.1), custom_call_target="tpu_custom_call" | custom-call | flops 201326592 | bytes 1572864 | tf_op jit(solution)/shard_map/project/pallas_call | solution.py:86
  11.7 1.0 %make_tables.1 = (bf16[2,4096]{1,0:T(2,128)(2,1)S(1)}, f32[2,16,128]{2,1,0:T(8,128)S(1)}, f32[32,128]{1,0:T(8,128)S(1)}, f32[256,128]{1,0:T(8,128)S(1)}) custom-call(bf16[2,8192]{1,0:T(2,128)(2,1)} %j_hbm.1, s32[3,32]{1,0:T(4,128)} %bitcast.3, f32[1,4]{1,0:T(1,128)} %bitcast.5, f32[1,256]{1,0:T(1,128)} %bitcast.4), custom_call_target="tpu_custom_call" | custom-call | flops 16384 | bytes 65536 | tf_op jit(solution)/shard_map/make_tables/pallas_call | solution.py:134
  12.7 0.9 %kernel_blocks.1.refs_0_ = bf16[6,256,512]{2,1,0:T(8,128)(2,1)S(1)} custom-call(bf16[2,4096]{1,0:T(2,128)(2,1)S(1)} %get-tuple-element.24.refs_0_.rest_0_.j_ref, f32[2,16,128]{2,1,0:T(8,128)S(1)} %get-tuple-element.25.refs_1_.rest_1_, f32[32,128]{1,0:T(8,128)S(1)} %get-tuple-element.26.refs_2_.rest_2_), custom_call_target="tpu_custom_call" | custom-call | flops 23592960 | bytes 1572864 | tf_op jit(solution)/shard_map/kernel_blocks/pallas_call | solution.py:313
  13.7 3.6 %collective-permute-done.1.refs_2_.refs_5_.refs_6_ = bf16[128,1024]{1,0:T(8,128)(2,1)S(1)} collective-permute-done((bf16[128,1024]{1,0:T(8,128)(2,1)S(1)}, bf16[128,1024]{1,0:T(8,128)(2,1)S(1)}, u32[]{:S(2)}, u32[]{:S(2)}) %collective-permute-start.1) | collective-permute-done | bytes 262176 | tf_op jit(solution)/shard_map/ppermute | solution.py:446
  17.7 1.1 %mix.8 = (f32[256,8192]{1,0:T(8,128)}, bf16[6,256,512]{2,1,0:T(8,128)(2,1)S(1)}) custom-call(bf16[128,768]{1,0:T(8,128)(2,1)S(1)} %smooth.4.s_ref, bf16[256,128]{1,0:T(8,128)(2,1)S(1)} %copy-done.2, f32[256,128]{1,0:T(8,128)S(1)} %get-tuple-element.27.g_ref, bf16[256,8192]{1,0:T(8,128)(2,1)S(1)} %copy-done.1, ...), custom_call_target="tpu_custom_call" | custom-call | flops 73924608 | bytes 2359296 | tf_op jit(solution)/shard_map/mix/pallas_call | solution.py:414
  19.1 1.2 %mix.9 = (f32[256,8192]{1,0:T(8,128)}, bf16[7,256,512]{2,1,0:T(8,128)(2,1)S(1)}) custom-call(bf16[128,768]{1,0:T(8,128)(2,1)S(1)} %collective-permute-done.2.s_ref, bf16[256,128]{1,0:T(8,128)(2,1)S(1)} %copy-done.2, f32[256,128]{1,0:T(8,128)S(1)} %get-tuple-element.27.g_ref, bf16[256,8192]{1,0:T(8,128)(2,1)S(1)} %copy-done.1, ...), custom_call_target="tpu_custom_call", output_to_operand_aliasing={{0}: (7, {})} | custom-call | flops 77856768 | bytes 2621440 | tf_op jit(solution)/shard_map/mix/pallas_call | solution.py:414
  20.4 5.5 %collective-permute-done.4.refs_3_.refs_4_ = bf16[128,1664]{1,0:T(8,128)(2,1)S(1)} collective-permute-done((bf16[128,1664]{1,0:T(8,128)(2,1)S(1)}, bf16[128,1664]{1,0:T(8,128)(2,1)S(1)}, u32[]{:S(2)}, u32[]{:S(2)}) %collective-permute-start.4) | collective-permute-done | bytes 426016 | tf_op jit(solution)/shard_map/ppermute | solution.py:446
  25.9 0.6 %smooth.5.s_ref = bf16[128,1664]{1,0:T(8,128)(2,1)S(1)} custom-call(bf16[6,256,512]{2,1,0:T(8,128)(2,1)S(1)} %get-tuple-element.28.refs_0_, bf16[7,256,512]{2,1,0:T(8,128)(2,1)S(1)} %get-tuple-element.30.refs_1_, bf16[128,1664]{1,0:T(8,128)(2,1)S(1)} %get-tuple-element.31.refs_2_.refs_3_, bf16[128,1664]{1,0:T(8,128)(2,1)S(1)} %collective-permute-done.4.refs_3_.refs_4_, ...), custom_call_target="tpu_custom_call" | custom-call | flops 218103808 | bytes 3407872 | tf_op jit(solution)/shard_map/smooth/pallas_call | solution.py:367
  26.6 1.8 %collective-permute-start.9 = (bf16[128,896]{1,0:T(8,128)(2,1)S(1)}, bf16[128,896]{1,0:T(8,128)(2,1)S(1)}, u32[]{:S(2)}, u32[]{:S(2)}) collective-permute-start(bf16[128,896]{1,0:T(8,128)(2,1)S(1)} %get-tuple-element.40.refs_3_.refs_1_), channel_id=1, source_target_pairs={{0,2},{1,3},{2,0},{3,1},{4,6},{5,7},{6,4},{7,5},{8,10},{9,11},{10,... | collective-permute-start | bytes 688136 | tf_op jit(solution)/shard_map/ppermute | solution.py:446
  28.6 4.3 %collective-permute-start.7 = (bf16[144,128]{1,0:T(8,128)(2,1)S(1)}, bf16[144,128]{1,0:T(8,128)(2,1)S(1)}, u32[]{:S(2)}, u32[]{:S(2)}) collective-permute-start(bf16[144,128]{1,0:T(8,128)(2,1)S(1)} %get-tuple-element.34), channel_id=1, source_target_pairs={{1,0},{4,1},{5,4},{8,5},{9,8},{12,9},{13,12},{16,13},{17,16},{20,1... | collective-permute-start | bytes 110600 | tf_op jit(solution)/shard_map/ppermute | solution.py:484
  32.9 1.6 %collective-permute-done.6.left_ref = bf16[144,128]{1,0:T(8,128)(2,1)S(1)} collective-permute-done((bf16[144,128]{1,0:T(8,128)(2,1)S(1)}, bf16[144,128]{1,0:T(8,128)(2,1)S(1)}, u32[]{:S(2)}, u32[]{:S(2)}) %collective-permute-start.6) | collective-permute-done | bytes 36896 | tf_op jit(solution)/shard_map/ppermute | solution.py:483
  35.0 1.5 %mix.10 = (f32[256,8192]{1,0:T(8,128)}, bf16[7,256,512]{2,1,0:T(8,128)(2,1)S(1)}) custom-call(bf16[128,1664]{1,0:T(8,128)(2,1)S(1)} %smooth.5.s_ref, bf16[256,128]{1,0:T(8,128)(2,1)S(1)} %copy-done.2, f32[256,128]{1,0:T(8,128)S(1)} %get-tuple-element.27.g_ref, bf16[256,8192]{1,0:T(8,128)(2,1)S(1)} %copy-done.1, ...), custom_call_target="tpu_custom_call", output_to_operand_aliasing={{0}: (7, {})} | custom-call | flops 136577024 | bytes 3538944 | tf_op jit(solution)/shard_map/mix/pallas_call | solution.py:414
  37.0 1.5 %mix.11 = (f32[256,8192]{1,0:T(8,128)}, bf16[6,256,512]{2,1,0:T(8,128)(2,1)S(1)}) custom-call(bf16[128,1664]{1,0:T(8,128)(2,1)S(1)} %collective-permute-done.5.s_ref, bf16[256,128]{1,0:T(8,128)(2,1)S(1)} %copy-done.2, f32[256,128]{1,0:T(8,128)S(1)} %get-tuple-element.27.g_ref, bf16[256,8192]{1,0:T(8,128)(2,1)S(1)} %copy-done.1, ...), custom_call_target="tpu_custom_call", output_to_operand_aliasing={{0}: (8, {})} | custom-call | flops 132644864 | bytes 3276800 | tf_op jit(solution)/shard_map/mix/pallas_call | solution.py:414
  38.5 1.4 %collective-permute-done.8.refs_2_ = bf16[128,640]{1,0:T(8,128)(2,1)S(1)} collective-permute-done((bf16[128,640]{1,0:T(8,128)(2,1)S(1)}, bf16[128,640]{1,0:T(8,128)(2,1)S(1)}, u32[]{:S(2)}, u32[]{:S(2)}) %collective-permute-start.8) | collective-permute-done | bytes 163872 | tf_op jit(solution)/shard_map/ppermute | solution.py:446
  40.4 1.2 %mix.12.rest_0_ = f32[256,8192]{1,0:T(8,128)} custom-call(bf16[128,896]{1,0:T(8,128)(2,1)S(1)} %smooth.7.s_ref, bf16[256,128]{1,0:T(8,128)(2,1)S(1)} %copy-done.2, f32[256,128]{1,0:T(8,128)S(1)} %get-tuple-element.27.g_ref, bf16[256,8192]{1,0:T(8,128)(2,1)S(1)} %copy-done.1, f32[256,8192]{1,0:T(8,128)} %get-tuple-element.42.rest_0_), custom_call_target="tpu_custom_call", output_to_operand_aliasing={{}: (4, {})} | custom-call | flops 58720256 | bytes 917504 | tf_op jit(solution)/shard_map/mix/pallas_call | solution.py:414
  41.6 1.2 %mix.13.rest_0_ = f32[256,8192]{1,0:T(8,128)} custom-call(bf16[128,896]{1,0:T(8,128)(2,1)S(1)} %collective-permute-done.11.s_ref, bf16[256,128]{1,0:T(8,128)(2,1)S(1)} %copy-done.2, f32[256,128]{1,0:T(8,128)S(1)} %get-tuple-element.27.g_ref, bf16[256,8192]{1,0:T(8,128)(2,1)S(1)} %copy-done.1, f32[256,8192]{1,0:T(8,128)} %mix.12.rest_0_), custom_call_target="tpu_custom_call", output_to_operand_aliasing={{}: (4, {})} | custom-call | flops 58720256 | bytes 917504 | tf_op jit(solution)/shard_map/mix/pallas_call | solution.py:414
  42.7 1.1 %mix.14.rest_0_ = f32[256,8192]{1,0:T(8,128)} custom-call(bf16[128,768]{1,0:T(8,128)(2,1)S(1)} %smooth.6.s_ref, bf16[256,128]{1,0:T(8,128)(2,1)S(1)} %copy-done.2, f32[256,128]{1,0:T(8,128)S(1)} %get-tuple-element.27.g_ref, bf16[256,8192]{1,0:T(8,128)(2,1)S(1)} %copy-done.1, f32[256,8192]{1,0:T(8,128)} %mix.13.rest_0_), custom_call_target="tpu_custom_call", output_to_operand_aliasing={{}: (4, {})} | custom-call | flops 50331648 | bytes 786432 | tf_op jit(solution)/shard_map/mix/pallas_call | solution.py:414
  43.8 1.1 %mix.15 = f32[256,8192]{1,0:T(8,128)} custom-call(bf16[128,768]{1,0:T(8,128)(2,1)S(1)} %collective-permute-done.10.s_ref, bf16[256,128]{1,0:T(8,128)(2,1)S(1)} %copy-done.2, f32[256,128]{1,0:T(8,128)S(1)} %get-tuple-element.27.g_ref, bf16[256,8192]{1,0:T(8,128)(2,1)S(1)} %copy-done.1, f32[256,8192]{1,0:T(8,128)} %mix.14.rest_0_), custom_call_target="tpu_custom_call", output_to_operand_aliasing={{}: (4, {})} | custom-call | flops 50331648 | bytes 786432 | tf_op jit(solution)/shard_map/mix/pallas_call | solution.py:414
  (28 shorter events, 3.0 us)
Async XLA Ops:
  0.0 2.2 %copy-start = (bf16[256,8192]{1,0:T(8,128)(2,1)S(1)}, bf16[256,8192]{1,0:T(8,128)(2,1)}, u32[]{:S(2)}) copy-start(bf16[256,8192]{1,0:T(8,128)(2,1)} %v_ref.15) | copy-start | bytes 12582916
  2.2 7.9 %copy-start.1 = (bf16[256,8192]{1,0:T(8,128)(2,1)S(1)}, bf16[256,8192]{1,0:T(8,128)(2,1)}, u32[]{:S(2)}) copy-start(bf16[256,8192]{1,0:T(8,128)(2,1)} %v_ref.15) | copy-start | bytes 12582916
  3.6 7.8 %collective-permute-start.3 = (bf16[128,3072]{1,0:T(8,128)(2,1)S(1)}, bf16[128,3072]{1,0:T(8,128)(2,1)S(1)}, u32[]{:S(2)}, u32[]{:S(2)}) collective-permute-start(bf16[128,3072]{1,0:T(8,128)(2,1)S(1)} %project.7), channel_id=1, source_target_pairs={{0,1},{1,0},{2,3},{3,2},{4,5},{5,4},{6,7},{7,6},{8,9},{9,8},{10,11... | collective-permute-start | bytes 2359304 | tf_op jit(solution)/shard_map/ppermute | solution.py:475
  5.5 12.2 %copy-start.2 = (bf16[256,128]{1,0:T(8,128)(2,1)S(1)}, bf16[256,128]{1,0:T(8,128)(2,1)}, u32[]{:S(2)}) copy-start(bf16[256,128]{1,0:T(8,128)(2,1)} %f_ref.15) | copy-start | bytes 196612
  5.6 1.6 %collective-permute-start = (bf16[128,1024]{1,0:T(8,128)(2,1)S(1)}, bf16[128,1024]{1,0:T(8,128)(2,1)S(1)}, u32[]{:S(2)}, u32[]{:S(2)}) collective-permute-start(bf16[128,1024]{1,0:T(8,128)(2,1)S(1)} %project.5), channel_id=1, source_target_pairs={{0,1},{1,0},{2,3},{3,2},{4,5},{5,4},{6,7},{7,6},{8,9},{9,8},{10,11... | collective-permute-start | bytes 786440 | tf_op jit(solution)/shard_map/ppermute | solution.py:468
  7.2 10.1 %collective-permute-start.1 = (bf16[128,1024]{1,0:T(8,128)(2,1)S(1)}, bf16[128,1024]{1,0:T(8,128)(2,1)S(1)}, u32[]{:S(2)}, u32[]{:S(2)}) collective-permute-start(bf16[128,1024]{1,0:T(8,128)(2,1)S(1)} %add_cores.2.refs_1_.refs_4_.first_ref.refs_5_), channel_id=1, source_target_pairs={{0,2},{1,3},{2,0},{3,1},{4,6},{5,7},{6,4},{7,5},{8,10},{9,11},{10,... | collective-permute-start | bytes 786440 | tf_op jit(solution)/shard_map/ppermute | solution.py:446
  11.6 14.3 %collective-permute-start.4 = (bf16[128,1664]{1,0:T(8,128)(2,1)S(1)}, bf16[128,1664]{1,0:T(8,128)(2,1)S(1)}, u32[]{:S(2)}, u32[]{:S(2)}) collective-permute-start(bf16[128,1664]{1,0:T(8,128)(2,1)S(1)} %get-tuple-element.31.refs_2_.refs_3_), channel_id=1, source_target_pairs={{0,2},{1,3},{2,0},{3,1},{4,6},{5,7},{6,4},{7,5},{8,10},{9,11},{10,... | collective-permute-start | bytes 1277960 | tf_op jit(solution)/shard_map/ppermute | solution.py:446
  17.6 1.5 %collective-permute-start.2 = (bf16[128,768]{1,0:T(8,128)(2,1)S(1)}, bf16[128,768]{1,0:T(8,128)(2,1)S(1)}, u32[]{:S(2)}, u32[]{:S(2)}) collective-permute-start(bf16[128,768]{1,0:T(8,128)(2,1)S(1)} %smooth.4.s_ref), channel_id=1, source_target_pairs={{0,1},{1,0},{2,3},{3,2},{4,5},{5,4},{6,7},{7,6},{8,9},{9,8},{10,11... | collective-permute-start | bytes 589832 | tf_op jit(solution)/shard_map/ppermute | solution.py:503
  26.5 10.5 %collective-permute-start.5 = (bf16[128,1664]{1,0:T(8,128)(2,1)S(1)}, bf16[128,1664]{1,0:T(8,128)(2,1)S(1)}, u32[]{:S(2)}, u32[]{:S(2)}) collective-permute-start(bf16[128,1664]{1,0:T(8,128)(2,1)S(1)} %smooth.5.s_ref), channel_id=1, source_target_pairs={{0,1},{1,0},{2,3},{3,2},{4,5},{5,4},{6,7},{7,6},{8,9},{9,8},{10,11... | collective-permute-start | bytes 1277960 | tf_op jit(solution)/shard_map/ppermute | solution.py:503
  26.6 10.0 %collective-permute-start.9 = (bf16[128,896]{1,0:T(8,128)(2,1)S(1)}, bf16[128,896]{1,0:T(8,128)(2,1)S(1)}, u32[]{:S(2)}, u32[]{:S(2)}) collective-permute-start(bf16[128,896]{1,0:T(8,128)(2,1)S(1)} %get-tuple-element.40.refs_3_.refs_1_), channel_id=1, source_target_pairs={{0,2},{1,3},{2,0},{3,1},{4,6},{5,7},{6,4},{7,5},{8,10},{9,11},{10,... | collective-permute-start | bytes 688136 | tf_op jit(solution)/shard_map/ppermute | solution.py:446
  28.4 6.1 %collective-permute-start.6 = (bf16[144,128]{1,0:T(8,128)(2,1)S(1)}, bf16[144,128]{1,0:T(8,128)(2,1)S(1)}, u32[]{:S(2)}, u32[]{:S(2)}) collective-permute-start(bf16[144,128]{1,0:T(8,128)(2,1)S(1)} %get-tuple-element.33), channel_id=1, source_target_pairs={{0,1},{1,4},{4,5},{5,8},{8,9},{9,12},{12,13},{13,16},{16,17},{17,2... | collective-permute-start | bytes 110600 | tf_op jit(solution)/shard_map/ppermute | solution.py:483
  28.6 5.9 %collective-permute-start.7 = (bf16[144,128]{1,0:T(8,128)(2,1)S(1)}, bf16[144,128]{1,0:T(8,128)(2,1)S(1)}, u32[]{:S(2)}, u32[]{:S(2)}) collective-permute-start(bf16[144,128]{1,0:T(8,128)(2,1)S(1)} %get-tuple-element.34), channel_id=1, source_target_pairs={{1,0},{4,1},{5,4},{8,5},{9,8},{12,9},{13,12},{16,13},{17,16},{20,1... | collective-permute-start | bytes 110600 | tf_op jit(solution)/shard_map/ppermute | solution.py:484
  34.6 5.4 %collective-permute-start.8 = (bf16[128,640]{1,0:T(8,128)(2,1)S(1)}, bf16[128,640]{1,0:T(8,128)(2,1)S(1)}, u32[]{:S(2)}, u32[]{:S(2)}) collective-permute-start(bf16[128,640]{1,0:T(8,128)(2,1)S(1)} %get-tuple-element.39.refs_1_), channel_id=1, source_target_pairs={{0,2},{1,3},{2,0},{3,1},{4,6},{5,7},{6,4},{7,5},{8,10},{9,11},{10,... | collective-permute-start | bytes 491528 | tf_op jit(solution)/shard_map/ppermute | solution.py:446
  36.9 4.6 %collective-permute-start.11 = (bf16[128,896]{1,0:T(8,128)(2,1)S(1)}, bf16[128,896]{1,0:T(8,128)(2,1)S(1)}, u32[]{:S(2)}, u32[]{:S(2)}) collective-permute-start(bf16[128,896]{1,0:T(8,128)(2,1)S(1)} %smooth.7.s_ref), channel_id=1, source_target_pairs={{0,1},{1,0},{2,3},{3,2},{4,5},{5,4},{6,7},{7,6},{8,9},{9,8},{10,11... | collective-permute-start | bytes 688136 | tf_op jit(solution)/shard_map/ppermute | solution.py:503
  40.3 3.5 %collective-permute-start.10 = (bf16[128,768]{1,0:T(8,128)(2,1)S(1)}, bf16[128,768]{1,0:T(8,128)(2,1)S(1)}, u32[]{:S(2)}, u32[]{:S(2)}) collective-permute-start(bf16[128,768]{1,0:T(8,128)(2,1)S(1)} %smooth.6.s_ref), channel_id=1, source_target_pairs={{0,1},{1,0},{2,3},{3,2},{4,5},{5,4},{6,7},{7,6},{8,9},{9,8},{10,11... | collective-permute-start | bytes 589832 | tf_op jit(solution)/shard_map/ppermute | solution.py:503

commit v3 on v2

--- a/solution.py
+++ b/solution.py
@@ -15,7 +15,7 @@
 STEP = 512
 EDGE_ROWS = 16
 MIB = 1 << 20
-CUTS = (7, 20, 27)
+CUTS = (6, 20, 26)
 
 VM = pl.BlockSpec(memory_space=pltpu.VMEM)
 HBM = pl.BlockSpec(memory_space=pltpu.HBM)
@@ -64,16 +64,18 @@
 
     def body(f_hbm, v_hbm, out, v_ref, f_ref, sems):
         side = core_of() if mine else 1 - core_of()
-        first = pltpu.make_async_copy(f_hbm, f_ref, sems.at[len(cuts)])
-        first.start()
+        first = None if resident else pltpu.make_async_copy(f_hbm, f_ref, sems.at[len(cuts)])
+        if first:
+            first.start()
         copies = [] if resident else [
             pltpu.make_async_copy(v_hbm.at[:, columns(at, size, side, span)], v_ref.at[:, pl.ds(place, size)], sems.at[i])
             for i, (at, place, size) in enumerate(cuts)
         ]
         for copy in copies:
             copy.start()
-        first.wait()
-        turned = f_ref[...].astype(jnp.float32).T.astype(jnp.bfloat16)
+        if first:
+            first.wait()
+        turned = (f_ref if first else f_hbm)[...].astype(jnp.float32).T.astype(jnp.bfloat16)
         for i, (at, place, size) in enumerate(cuts):
             s = slice(place, place + size)
             if resident:
@@ -86,7 +88,7 @@
     return pl.pallas_call(
         body,
         out_shape=shape((ranks, width), kind),
-        in_specs=[HBM, VM if resident else HBM],
+        in_specs=[VM, VM] if resident else [HBM, HBM],
         out_specs=VM,
         scratch_shapes=[
             pltpu.VMEM((16, GROUP) if resident else (tasks, width), values.dtype),
@@ -96,7 +98,7 @@
         compiler_params=grant(14),
         cost_estimate=cost(2 * tasks * ranks * width, tasks * width * 2),
         name="project",
-    )(in_hbm(factors), values if resident else in_hbm(values))
+    )(*((factors, values) if resident else (in_hbm(factors), in_hbm(values))))
 
 
 def make_tables(jitter, neighbours, scales, nugget):

time: 45.2 us -> 50 us (1.11)
  waiting for transfers between devices: 12.6 us -> 16.1 us
  starting transfers between devices: 10.7 us -> 12.7 us
  Pallas kernels: 19.2 us -> 17.6 us
  local copies, waits for them, and re-layouts: 2.2 us -> 3.05 us
    ppermute x4, waiting for transfers between devices: 10.5 us -> 15.9 us  [sum_fields(): other = lax.ppermute(share, 'task', partners(size, bit))]
    ppermute x1, waiting for transfers between devices: 1.64 us -> 0.01 us  [steps_of(): from_left = lax.ppermute(right_edge, ('site', 'task'), up)]
    pallas_call x4, Pallas kernels: 5.4 us -> 3.81 us  [project(): pl.pallas_call(body, out_shape=shape((ranks, width), kind), in_specs=[VM,...]
    ppermute x4, starting transfers between devices: 5.27 us -> 6.25 us  [sum_fields(): other = lax.ppermute(share, 'task', partners(size, bit))]
    unnamed x6 -> x12, local copies, waits for them, and re-layouts: 2.2 us -> 3.05 us
    ppermute x4, starting transfers between devices: 0.28 us -> 1.09 us  [steps_of(): other = lax.ppermute(smoothed, 'task', partners(peers, 1))]
  transfers between devices with their start and end apart: 12 -> 12, of which waited for: 6 -> 5; matrix products, arithmetic and copies ran while one was open for 0% -> 0% of each run, Pallas kernels for 36% -> 30%
where the time goes in v3:
time: 50 us; the launch traced here: 49.8 us
  Pallas kernels  17.6 us (35%)
  waiting for transfers between devices  16.1 us (32%)
  starting transfers between devices  12.7 us (25%)
  local copies, waits for them, and re-layouts  3.05 us (6%)
    ppermute x4, waiting for transfers between devices, sum_fields(): other = lax.ppermute(share, 'task', partners(size, bit))  15.9 us
    pallas_call x8, Pallas kernels, mix(): pl.pallas_call(body, out_shape=out, in_specs=specs, out_specs=out_specs,...  9.99 us
    ppermute x4, starting transfers between devices, sum_fields(): other = lax.ppermute(share, 'task', partners(size, bit))  6.25 us
    ppermute x1, starting transfers between devices, steps_of(): from_right = lax.ppermute(left_edge, ('site', 'task'), down)  4.42 us
    pallas_call x4, Pallas kernels, project(): pl.pallas_call(body, out_shape=shape((ranks, width), kind), in_specs=[VM,...  3.81 us
    unnamed x12, local copies, waits for them, and re-layouts  3.05 us
    pallas_call x4, Pallas kernels, smooth(): pl.pallas_call(body, out_shape=shape((half, count), jnp.bfloat16), in_spe...  1.77 us
    ppermute x4, starting transfers between devices, steps_of(): other = lax.ppermute(smoothed, 'task', partners(peers, 1))  1.09 us
  transfers between devices with their start and end apart: 12, of which 5 were waited for; matrix products, arithmetic and copies ran while one was open for 0% of the time, Pallas kernels for 30%

profile of v3, /device:TPU:0, one launch (start us, length us, event | category | flops | bytes accessed | tf_op | source)
XLA Modules:
  0.0 49.8 jit_solution(7837245567134792942)
XLA Ops:
  0.0 2.2 %copy-done = bf16[256,8192]{1,0:T(8,128)(2,1)S(1)} copy-done((bf16[256,8192]{1,0:T(8,128)(2,1)S(1)}, bf16[256,8192]{1,0:T(8,128)(2,1)}, u32[]{:S(2)}) %copy-start) | copy-done | bytes 4194328
  2.2 0.8 %copy-done.3 = bf16[256,128]{1,0:T(8,128)(2,1)S(1)} copy-done((bf16[256,128]{1,0:T(8,128)(2,1)S(1)}, bf16[256,128]{1,0:T(8,128)(2,1)}, u32[]{:S(2)}) %copy-start.3) | copy-done | bytes 65560
  3.5 0.6 %collective-permute-start.3 = (bf16[128,3200]{1,0:T(8,128)(2,1)S(1)}, bf16[128,3200]{1,0:T(8,128)(2,1)S(1)}, u32[]{:S(2)}, u32[]{:S(2)}) collective-permute-start(bf16[128,3200]{1,0:T(8,128)(2,1)S(1)} %project.7), channel_id=1, source_target_pairs={{0,1},{1,0},{2,3},{3,2},{4,5},{5,4},{6,7},{7,6},{8,9},{9,8},{10,11... | collective-permute-start | bytes 2457608 | tf_op jit(solution)/shard_map/ppermute | solution.py:477
  4.1 1.5 %project.5 = bf16[128,896]{1,0:T(8,128)(2,1)S(1)} custom-call(bf16[256,128]{1,0:T(8,128)(2,1)} %f_ref.15, bf16[256,8192]{1,0:T(8,128)(2,1)} %v_ref.15), custom_call_target="tpu_custom_call" | custom-call | flops 58720256 | bytes 458752 | tf_op jit(solution)/shard_map/project/pallas_call | solution.py:88
  6.4 2.8 %collective-permute-start.4 = (bf16[128,1792]{1,0:T(8,128)(2,1)S(1)}, bf16[128,1792]{1,0:T(8,128)(2,1)S(1)}, u32[]{:S(2)}, u32[]{:S(2)}) collective-permute-start(bf16[128,1792]{1,0:T(8,128)(2,1)S(1)} %get-tuple-element.31.refs_2_.refs_3_), channel_id=1, source_target_pairs={{0,2},{1,3},{2,0},{3,1},{4,6},{5,7},{6,4},{7,5},{8,10},{9,11},{10,... | collective-permute-start | bytes 1376264 | tf_op jit(solution)/shard_map/ppermute | solution.py:448
  9.3 1.3 %project.4.own_ref = f32[128,896]{1,0:T(8,128)S(1)} custom-call(bf16[256,128]{1,0:T(8,128)(2,1)} %f_ref.15, bf16[256,8192]{1,0:T(8,128)(2,1)} %v_ref.15), custom_call_target="tpu_custom_call" | custom-call | flops 58720256 | bytes 458752 | tf_op jit(solution)/shard_map/project/pallas_call | solution.py:88
  10.8 1.0 %make_tables.1 = (bf16[2,4096]{1,0:T(2,128)(2,1)S(1)}, f32[2,16,128]{2,1,0:T(8,128)S(1)}, f32[32,128]{1,0:T(8,128)S(1)}, f32[256,128]{1,0:T(8,128)S(1)}) custom-call(bf16[2,8192]{1,0:T(2,128)(2,1)} %j_hbm.1, s32[3,32]{1,0:T(4,128)} %bitcast.3, f32[1,4]{1,0:T(1,128)} %bitcast.5, f32[1,256]{1,0:T(1,128)} %bitcast.4), custom_call_target="tpu_custom_call" | custom-call | flops 16384 | bytes 65536 | tf_op jit(solution)/shard_map/make_tables/pallas_call | solution.py:136
  11.9 0.8 %kernel_blocks.1.refs_0_ = bf16[5,256,512]{2,1,0:T(8,128)(2,1)S(1)} custom-call(bf16[2,4096]{1,0:T(2,128)(2,1)S(1)} %get-tuple-element.24.refs_0_.rest_0_.j_ref, f32[2,16,128]{2,1,0:T(8,128)S(1)} %get-tuple-element.25.refs_1_.rest_1_, f32[32,128]{1,0:T(8,128)S(1)} %get-tuple-element.26.refs_2_.rest_2_), custom_call_target="tpu_custom_call" | custom-call | flops 19660800 | bytes 1310720 | tf_op jit(solution)/shard_map/kernel_blocks/pallas_call | solution.py:315
  12.7 12.4 %collective-permute-done.1.refs_2_.refs_5_.refs_6_ = bf16[128,896]{1,0:T(8,128)(2,1)S(1)} collective-permute-done((bf16[128,896]{1,0:T(8,128)(2,1)S(1)}, bf16[128,896]{1,0:T(8,128)(2,1)S(1)}, u32[]{:S(2)}, u32[]{:S(2)}) %collective-permute-start.1) | collective-permute-done | bytes 229408 | tf_op jit(solution)/shard_map/ppermute | solution.py:448
  25.5 1.2 %mix.8 = (f32[256,8192]{1,0:T(8,128)}, bf16[7,256,512]{2,1,0:T(8,128)(2,1)S(1)}) custom-call(bf16[128,640]{1,0:T(8,128)(2,1)S(1)} %smooth.4.s_ref, bf16[256,128]{1,0:T(8,128)(2,1)S(1)} %copy-done.5, f32[256,128]{1,0:T(8,128)S(1)} %get-tuple-element.27.g_ref, bf16[256,8192]{1,0:T(8,128)(2,1)S(1)} %copy-done.2, ...), custom_call_target="tpu_custom_call" | custom-call | flops 69468160 | bytes 2490368 | tf_op jit(solution)/shard_map/mix/pallas_call | solution.py:416
  26.9 1.2 %mix.9 = (f32[256,8192]{1,0:T(8,128)}, bf16[7,256,512]{2,1,0:T(8,128)(2,1)S(1)}) custom-call(bf16[128,640]{1,0:T(8,128)(2,1)S(1)} %collective-permute-done.2.s_ref, bf16[256,128]{1,0:T(8,128)(2,1)S(1)} %copy-done.5, f32[256,128]{1,0:T(8,128)S(1)} %get-tuple-element.27.g_ref, bf16[256,8192]{1,0:T(8,128)(2,1)S(1)} %copy-done.2, ...), custom_call_target="tpu_custom_call", output_to_operand_aliasing={{0}: (7, {})} | custom-call | flops 69468160 | bytes 2490368 | tf_op jit(solution)/shard_map/mix/pallas_call | solution.py:416
  28.1 0.6 %smooth.5.s_ref = bf16[128,1792]{1,0:T(8,128)(2,1)S(1)} custom-call(bf16[7,256,512]{2,1,0:T(8,128)(2,1)S(1)} %get-tuple-element.28.refs_0_, bf16[7,256,512]{2,1,0:T(8,128)(2,1)S(1)} %get-tuple-element.30.refs_1_, bf16[128,1792]{1,0:T(8,128)(2,1)S(1)} %get-tuple-element.31.refs_2_.refs_3_, bf16[128,1792]{1,0:T(8,128)(2,1)S(1)} %collective-permute-done.4.refs_3_.refs_4_, ...), custom_call_target="tpu_custom_call" | custom-call | flops 234881024 | bytes 3670016 | tf_op jit(solution)/shard_map/smooth/pallas_call | solution.py:369
  29.4 4.4 %collective-permute-start.7 = (bf16[144,128]{1,0:T(8,128)(2,1)S(1)}, bf16[144,128]{1,0:T(8,128)(2,1)S(1)}, u32[]{:S(2)}, u32[]{:S(2)}) collective-permute-start(bf16[144,128]{1,0:T(8,128)(2,1)S(1)} %get-tuple-element.34), channel_id=1, source_target_pairs={{1,0},{4,1},{5,4},{8,5},{9,8},{12,9},{13,12},{16,13},{17,16},{20,1... | collective-permute-start | bytes 110600 | tf_op jit(solution)/shard_map/ppermute | solution.py:486
  33.8 1.6 %collective-permute-start.9 = (bf16[128,768]{1,0:T(8,128)(2,1)S(1)}, bf16[128,768]{1,0:T(8,128)(2,1)S(1)}, u32[]{:S(2)}, u32[]{:S(2)}) collective-permute-start(bf16[128,768]{1,0:T(8,128)(2,1)S(1)} %get-tuple-element.40.refs_3_.refs_1_), channel_id=1, source_target_pairs={{0,2},{1,3},{2,0},{3,1},{4,6},{5,7},{6,4},{7,5},{8,10},{9,11},{10,... | collective-permute-start | bytes 589832 | tf_op jit(solution)/shard_map/ppermute | solution.py:448
  35.5 1.6 %collective-permute-start.8 = (bf16[128,768]{1,0:T(8,128)(2,1)S(1)}, bf16[128,768]{1,0:T(8,128)(2,1)S(1)}, u32[]{:S(2)}, u32[]{:S(2)}) collective-permute-start(bf16[128,768]{1,0:T(8,128)(2,1)S(1)} %get-tuple-element.39.refs_1_), channel_id=1, source_target_pairs={{0,2},{1,3},{2,0},{3,1},{4,6},{5,7},{6,4},{7,5},{8,10},{9,11},{10,... | collective-permute-start | bytes 589832 | tf_op jit(solution)/shard_map/ppermute | solution.py:448
  37.2 1.5 %mix.10 = (f32[256,8192]{1,0:T(8,128)}, bf16[6,256,512]{2,1,0:T(8,128)(2,1)S(1)}) custom-call(bf16[128,1792]{1,0:T(8,128)(2,1)S(1)} %smooth.5.s_ref, bf16[256,128]{1,0:T(8,128)(2,1)S(1)} %copy-done.5, f32[256,128]{1,0:T(8,128)S(1)} %get-tuple-element.27.g_ref, bf16[256,8192]{1,0:T(8,128)(2,1)S(1)} %copy-done.2, ...), custom_call_target="tpu_custom_call", output_to_operand_aliasing={{0}: (7, {})} | custom-call | flops 141033472 | bytes 3407872 | tf_op jit(solution)/shard_map/mix/pallas_call | solution.py:416
  38.7 1.5 %mix.11 = (f32[256,8192]{1,0:T(8,128)}, bf16[7,256,512]{2,1,0:T(8,128)(2,1)S(1)}) custom-call(bf16[128,1792]{1,0:T(8,128)(2,1)S(1)} %collective-permute-done.5.s_ref, bf16[256,128]{1,0:T(8,128)(2,1)S(1)} %copy-done.5, f32[256,128]{1,0:T(8,128)S(1)} %get-tuple-element.27.g_ref, bf16[256,8192]{1,0:T(8,128)(2,1)S(1)} %copy-done.2, ...), custom_call_target="tpu_custom_call", output_to_operand_aliasing={{0}: (8, {})} | custom-call | flops 144965632 | bytes 3670016 | tf_op jit(solution)/shard_map/mix/pallas_call | solution.py:416
  40.3 1.3 %collective-permute-done.9.refs_4_.refs_2_ = bf16[128,768]{1,0:T(8,128)(2,1)S(1)} collective-permute-done((bf16[128,768]{1,0:T(8,128)(2,1)S(1)}, bf16[128,768]{1,0:T(8,128)(2,1)S(1)}, u32[]{:S(2)}, u32[]{:S(2)}) %collective-permute-start.9) | collective-permute-done | bytes 196640 | tf_op jit(solution)/shard_map/ppermute | solution.py:448
  41.6 2.1 %collective-permute-done.8.refs_2_ = bf16[128,768]{1,0:T(8,128)(2,1)S(1)} collective-permute-done((bf16[128,768]{1,0:T(8,128)(2,1)S(1)}, bf16[128,768]{1,0:T(8,128)(2,1)S(1)}, u32[]{:S(2)}, u32[]{:S(2)}) %collective-permute-start.8) | collective-permute-done | bytes 196640 | tf_op jit(solution)/shard_map/ppermute | solution.py:448
  44.6 0.6 %collective-permute-start.11 = (bf16[128,768]{1,0:T(8,128)(2,1)S(1)}, bf16[128,768]{1,0:T(8,128)(2,1)S(1)}, u32[]{:S(2)}, u32[]{:S(2)}) collective-permute-start(bf16[128,768]{1,0:T(8,128)(2,1)S(1)} %smooth.7.s_ref), channel_id=1, source_target_pairs={{0,1},{1,0},{2,3},{3,2},{4,5},{5,4},{6,7},{7,6},{8,9},{9,8},{10,11... | collective-permute-start | bytes 589832 | tf_op jit(solution)/shard_map/ppermute | solution.py:505
  45.2 1.1 %mix.12.rest_0_ = f32[256,8192]{1,0:T(8,128)} custom-call(bf16[128,768]{1,0:T(8,128)(2,1)S(1)} %smooth.7.s_ref, bf16[256,128]{1,0:T(8,128)(2,1)S(1)} %copy-done.5, f32[256,128]{1,0:T(8,128)S(1)} %get-tuple-element.27.g_ref, bf16[256,8192]{1,0:T(8,128)(2,1)S(1)} %copy-done.2, f32[256,8192]{1,0:T(8,128)} %get-tuple-element.42.rest_0_), custom_call_target="tpu_custom_call", output_to_operand_aliasing={{}: (4, {})} | custom-call | flops 50331648 | bytes 786432 | tf_op jit(solution)/shard_map/mix/pallas_call | solution.py:416
  46.3 1.1 %mix.13.rest_0_ = f32[256,8192]{1,0:T(8,128)} custom-call(bf16[128,768]{1,0:T(8,128)(2,1)S(1)} %collective-permute-done.11.s_ref, bf16[256,128]{1,0:T(8,128)(2,1)S(1)} %copy-done.5, f32[256,128]{1,0:T(8,128)S(1)} %get-tuple-element.27.g_ref, bf16[256,8192]{1,0:T(8,128)(2,1)S(1)} %copy-done.2, f32[256,8192]{1,0:T(8,128)} %mix.12.rest_0_), custom_call_target="tpu_custom_call", output_to_operand_aliasing={{}: (4, {})} | custom-call | flops 50331648 | bytes 786432 | tf_op jit(solution)/shard_map/mix/pallas_call | solution.py:416
  47.4 1.2 %mix.14.rest_0_ = f32[256,8192]{1,0:T(8,128)} custom-call(bf16[128,896]{1,0:T(8,128)(2,1)S(1)} %smooth.6.s_ref, bf16[256,128]{1,0:T(8,128)(2,1)S(1)} %copy-done.5, f32[256,128]{1,0:T(8,128)S(1)} %get-tuple-element.27.g_ref, bf16[256,8192]{1,0:T(8,128)(2,1)S(1)} %copy-done.2, f32[256,8192]{1,0:T(8,128)} %mix.13.rest_0_), custom_call_target="tpu_custom_call", output_to_operand_aliasing={{}: (4, {})} | custom-call | flops 58720256 | bytes 917504 | tf_op jit(solution)/shard_map/mix/pallas_call | solution.py:416
  48.6 1.2 %mix.15 = f32[256,8192]{1,0:T(8,128)} custom-call(bf16[128,896]{1,0:T(8,128)(2,1)S(1)} %collective-permute-done.10.s_ref, bf16[256,128]{1,0:T(8,128)(2,1)S(1)} %copy-done.5, f32[256,128]{1,0:T(8,128)S(1)} %get-tuple-element.27.g_ref, bf16[256,8192]{1,0:T(8,128)(2,1)S(1)} %copy-done.2, f32[256,8192]{1,0:T(8,128)} %mix.14.rest_0_), custom_call_target="tpu_custom_call", output_to_operand_aliasing={{}: (4, {})} | custom-call | flops 58720256 | bytes 917504 | tf_op jit(solution)/shard_map/mix/pallas_call | solution.py:416
  (34 shorter events, 3.7 us)
Async XLA Ops:
  0.0 2.2 %copy-start = (bf16[256,8192]{1,0:T(8,128)(2,1)S(1)}, bf16[256,8192]{1,0:T(8,128)(2,1)}, u32[]{:S(2)}) copy-start(bf16[256,8192]{1,0:T(8,128)(2,1)} %v_ref.15) | copy-start | bytes 12582916
  2.2 0.8 %copy-start.3 = (bf16[256,128]{1,0:T(8,128)(2,1)S(1)}, bf16[256,128]{1,0:T(8,128)(2,1)}, u32[]{:S(2)}) copy-start(bf16[256,128]{1,0:T(8,128)(2,1)} %f_ref.15) | copy-start | bytes 196612
  3.0 2.8 %copy-start.1 = (bf16[256,8192]{1,0:T(8,128)(2,1)S(1)}, bf16[256,8192]{1,0:T(8,128)(2,1)}, u32[]{:S(2)}) copy-start(bf16[256,8192]{1,0:T(8,128)(2,1)} %v_ref.15) | copy-start | bytes 12582916
  3.0 2.8 %copy-start.4 = (bf16[256,128]{1,0:T(8,128)(2,1)S(1)}, bf16[256,128]{1,0:T(8,128)(2,1)}, u32[]{:S(2)}) copy-start(bf16[256,128]{1,0:T(8,128)(2,1)} %f_ref.15) | copy-start | bytes 196612
  3.5 2.8 %collective-permute-start.3 = (bf16[128,3200]{1,0:T(8,128)(2,1)S(1)}, bf16[128,3200]{1,0:T(8,128)(2,1)S(1)}, u32[]{:S(2)}, u32[]{:S(2)}) collective-permute-start(bf16[128,3200]{1,0:T(8,128)(2,1)S(1)} %project.7), channel_id=1, source_target_pairs={{0,1},{1,0},{2,3},{3,2},{4,5},{5,4},{6,7},{7,6},{8,9},{9,8},{10,11... | collective-permute-start | bytes 2457608 | tf_op jit(solution)/shard_map/ppermute | solution.py:477
  5.6 19.9 %copy-start.2 = (bf16[256,8192]{1,0:T(8,128)(2,1)S(1)}, bf16[256,8192]{1,0:T(8,128)(2,1)}, u32[]{:S(2)}) copy-start(bf16[256,8192]{1,0:T(8,128)(2,1)} %v_ref.15) | copy-start | bytes 12582916
  5.6 19.9 %copy-start.5 = (bf16[256,128]{1,0:T(8,128)(2,1)S(1)}, bf16[256,128]{1,0:T(8,128)(2,1)}, u32[]{:S(2)}) copy-start(bf16[256,128]{1,0:T(8,128)(2,1)} %f_ref.15) | copy-start | bytes 196612
  5.6 4.9 %collective-permute-start = (bf16[128,896]{1,0:T(8,128)(2,1)S(1)}, bf16[128,896]{1,0:T(8,128)(2,1)S(1)}, u32[]{:S(2)}, u32[]{:S(2)}) collective-permute-start(bf16[128,896]{1,0:T(8,128)(2,1)S(1)} %project.5), channel_id=1, source_target_pairs={{0,1},{1,0},{2,3},{3,2},{4,5},{5,4},{6,7},{7,6},{8,9},{9,8},{10,11... | collective-permute-start | bytes 688136 | tf_op jit(solution)/shard_map/ppermute | solution.py:470
  6.4 21.7 %collective-permute-start.4 = (bf16[128,1792]{1,0:T(8,128)(2,1)S(1)}, bf16[128,1792]{1,0:T(8,128)(2,1)S(1)}, u32[]{:S(2)}, u32[]{:S(2)}) collective-permute-start(bf16[128,1792]{1,0:T(8,128)(2,1)S(1)} %get-tuple-element.31.refs_2_.refs_3_), channel_id=1, source_target_pairs={{0,2},{1,3},{2,0},{3,1},{4,6},{5,7},{6,4},{7,5},{8,10},{9,11},{10,... | collective-permute-start | bytes 1376264 | tf_op jit(solution)/shard_map/ppermute | solution.py:448
  10.6 14.5 %collective-permute-start.1 = (bf16[128,896]{1,0:T(8,128)(2,1)S(1)}, bf16[128,896]{1,0:T(8,128)(2,1)S(1)}, u32[]{:S(2)}, u32[]{:S(2)}) collective-permute-start(bf16[128,896]{1,0:T(8,128)(2,1)S(1)} %add_cores.2.refs_1_.refs_4_.first_ref.refs_5_), channel_id=1, source_target_pairs={{0,2},{1,3},{2,0},{3,1},{4,6},{5,7},{6,4},{7,5},{8,10},{9,11},{10,... | collective-permute-start | bytes 688136 | tf_op jit(solution)/shard_map/ppermute | solution.py:448
  25.4 1.5 %collective-permute-start.2 = (bf16[128,640]{1,0:T(8,128)(2,1)S(1)}, bf16[128,640]{1,0:T(8,128)(2,1)S(1)}, u32[]{:S(2)}, u32[]{:S(2)}) collective-permute-start(bf16[128,640]{1,0:T(8,128)(2,1)S(1)} %smooth.4.s_ref), channel_id=1, source_target_pairs={{0,1},{1,0},{2,3},{3,2},{4,5},{5,4},{6,7},{7,6},{8,9},{9,8},{10,11... | collective-permute-start | bytes 491528 | tf_op jit(solution)/shard_map/ppermute | solution.py:505
  28.8 9.9 %collective-permute-start.5 = (bf16[128,1792]{1,0:T(8,128)(2,1)S(1)}, bf16[128,1792]{1,0:T(8,128)(2,1)S(1)}, u32[]{:S(2)}, u32[]{:S(2)}) collective-permute-start(bf16[128,1792]{1,0:T(8,128)(2,1)S(1)} %smooth.5.s_ref), channel_id=1, source_target_pairs={{0,1},{1,0},{2,3},{3,2},{4,5},{5,4},{6,7},{7,6},{8,9},{9,8},{10,11... | collective-permute-start | bytes 1376264 | tf_op jit(solution)/shard_map/ppermute | solution.py:505
  29.2 6.2 %collective-permute-start.6 = (bf16[144,128]{1,0:T(8,128)(2,1)S(1)}, bf16[144,128]{1,0:T(8,128)(2,1)S(1)}, u32[]{:S(2)}, u32[]{:S(2)}) collective-permute-start(bf16[144,128]{1,0:T(8,128)(2,1)S(1)} %get-tuple-element.33), channel_id=1, source_target_pairs={{0,1},{1,4},{4,5},{5,8},{8,9},{9,12},{12,13},{13,16},{16,17},{17,2... | collective-permute-start | bytes 110600 | tf_op jit(solution)/shard_map/ppermute | solution.py:485
  29.4 6.1 %collective-permute-start.7 = (bf16[144,128]{1,0:T(8,128)(2,1)S(1)}, bf16[144,128]{1,0:T(8,128)(2,1)S(1)}, u32[]{:S(2)}, u32[]{:S(2)}) collective-permute-start(bf16[144,128]{1,0:T(8,128)(2,1)S(1)} %get-tuple-element.34), channel_id=1, source_target_pairs={{1,0},{4,1},{5,4},{8,5},{9,8},{12,9},{13,12},{16,13},{17,16},{20,1... | collective-permute-start | bytes 110600 | tf_op jit(solution)/shard_map/ppermute | solution.py:486
  33.8 7.8 %collective-permute-start.9 = (bf16[128,768]{1,0:T(8,128)(2,1)S(1)}, bf16[128,768]{1,0:T(8,128)(2,1)S(1)}, u32[]{:S(2)}, u32[]{:S(2)}) collective-permute-start(bf16[128,768]{1,0:T(8,128)(2,1)S(1)} %get-tuple-element.40.refs_3_.refs_1_), channel_id=1, source_target_pairs={{0,2},{1,3},{2,0},{3,1},{4,6},{5,7},{6,4},{7,5},{8,10},{9,11},{10,... | collective-permute-start | bytes 589832 | tf_op jit(solution)/shard_map/ppermute | solution.py:448
  35.5 8.2 %collective-permute-start.8 = (bf16[128,768]{1,0:T(8,128)(2,1)S(1)}, bf16[128,768]{1,0:T(8,128)(2,1)S(1)}, u32[]{:S(2)}, u32[]{:S(2)}) collective-permute-start(bf16[128,768]{1,0:T(8,128)(2,1)S(1)} %get-tuple-element.39.refs_1_), channel_id=1, source_target_pairs={{0,2},{1,3},{2,0},{3,1},{4,6},{5,7},{6,4},{7,5},{8,10},{9,11},{10,... | collective-permute-start | bytes 589832 | tf_op jit(solution)/shard_map/ppermute | solution.py:448
  44.2 4.4 %collective-permute-start.10 = (bf16[128,896]{1,0:T(8,128)(2,1)S(1)}, bf16[128,896]{1,0:T(8,128)(2,1)S(1)}, u32[]{:S(2)}, u32[]{:S(2)}) collective-permute-start(bf16[128,896]{1,0:T(8,128)(2,1)S(1)} %smooth.6.s_ref), channel_id=1, source_target_pairs={{0,1},{1,0},{2,3},{3,2},{4,5},{5,4},{6,7},{7,6},{8,9},{9,8},{10,11... | collective-permute-start | bytes 688136 | tf_op jit(solution)/shard_map/ppermute | solution.py:505
  44.6 1.7 %collective-permute-start.11 = (bf16[128,768]{1,0:T(8,128)(2,1)S(1)}, bf16[128,768]{1,0:T(8,128)(2,1)S(1)}, u32[]{:S(2)}, u32[]{:S(2)}) collective-permute-start(bf16[128,768]{1,0:T(8,128)(2,1)S(1)} %smooth.7.s_ref), channel_id=1, source_target_pairs={{0,1},{1,0},{2,3},{3,2},{4,5},{5,4},{6,7},{7,6},{8,9},{9,8},{10,11... | collective-permute-start | bytes 589832 | tf_op jit(solution)/shard_map/ppermute | solution.py:505
